TPU v7x, 32 devices: a whole 2x2x4 slice. The times are simulated.
32 devices in a mesh: grp: 2 (over y), gx: 8 (over z, x), rep: 2 (over core).
Axes of the slice: x: 2, y: 2, z: 4, core: 2. Of those that a mesh axis runs over, the one named last changes fastest.
Arguments:
- fields: bfloat16 [4, 128, 32, 128, 128], P(('grp', 'rep'), 'gx'), parts along dimension 0, may hold values from -6 to 6
- targets: bfloat16 [4, 128, 3, 128, 128], P(('grp', 'rep'), 'gx'), parts along dimension 0, may hold values from -3 to 3
- multipliers: int32 [4, 128, 128, 128], P(('grp', 'rep'), 'gx'), parts along dimension 0, may hold values from -256 to 256
- local_weight: bfloat16 [32, 32], replicated, may hold values from -1 to 1
- proj_weight: bfloat16 [32, 3], replicated, may hold values from -1 to 1
- spectral_weight: bfloat16 [16, 256, 2, 32, 32], P('rep', 'gx'), may hold values from -9 to 9
Outputs:
- new_multipliers: float32 [4, 128, 128, 128], P(('grp', 'rep'), 'gx'), parts along dimension 0
- grad_spectral: float32 [32, 256, 2, 32, 32], P(('grp', 'rep'), 'gx'), parts along dimension 0
- grad_local: float32 [64, 32], P('grp'), parts along dimension 0
- grad_proj: float32 [64, 3], P('grp'), parts along dimension 0
- loss: float32 [2], P('grp'), parts along dimension 0
There are 2 independent parts, one for each index of `grp`. A program takes and returns all parts, laid end to end along the dimension named above; an argument that names none is the same for every part. Nothing has to cross between parts.
All inputs are finite; a program needn't handle non-finite values.
Results may differ from a plain program's by a relative error of at most 0.0005.
The roundings to bfloat16 on the way count: a program that leaves them out, or rounds other values in their place, can miss the bound.
Values may be sent and summed in bfloat16 or wider, within the bound.
A program may use at most 256 MiB of HBM per device.

v0:
```python
import math

import jax
import jax.numpy as jnp
from jax import lax
from jax.sharding import PartitionSpec as P

NX = 128
NY = 128
NZ = 128
MX = 16
MY = 16
MZ = 16


penalty_weight = 0.5
precise = lax.Precision.HIGHEST


def extended(value, sides, width):
    for axis, dim in sides:
        count, length = (lax.axis_size(axis), value.shape[dim])
        up = [(i, (i + 1) % count) for i in range(count)]
        down = [(j, i) for i, j in up]
        last = lax.slice_in_dim(value, length - width, length, axis=dim)
        initial = lax.slice_in_dim(value, 0, width, axis=dim)
        before = lax.ppermute(last, axis, up)
        after = lax.ppermute(initial, axis, down)
        value = jnp.concatenate([before, value, after], axis=dim)
    return value


def as_sent(value):

    def short(part):
        return part.astype(jnp.bfloat16) if part.dtype == jnp.float32 else part

    return jax.tree.map(short, value)


def mode_numbers(count):
    position = jnp.arange(count, dtype=jnp.int32)
    return jnp.where(position < count // 2, position, position - count)


def fourier_tables(length, count):
    cells = jnp.arange(length, dtype=jnp.int32)
    phase = jnp.mod(cells[:, None] * mode_numbers(count)[None, :], length)
    angle = phase.astype(jnp.float32) * (2.0 * math.pi / length)
    return (jnp.cos(angle), jnp.sin(angle))


def to_last(values, table):
    return jnp.einsum("...kz,zm->...km", values, table, precision=precise)


def from_last(values, table):
    return jnp.einsum("...km,zm->...kz", values, table, precision=precise)


def forward_plane(field):
    cos_y, sin_y = fourier_tables(NY, MY)
    lookup_table_y = jnp.stack([cos_y, -sin_y], axis=1).astype(jnp.bfloat16)
    partial_value = jnp.einsum(
        "...cyz,yrk->...crkz", field, lookup_table_y, preferred_element_type=jnp.float32
    )
    cos_z, sin_z = fourier_tables(NZ, MZ)
    real_part = partial_value[..., 0, :, :]
    imag_part = partial_value[..., 1, :, :]
    spec_re = to_last(real_part, cos_z) + to_last(imag_part, sin_z)
    spec_im = to_last(imag_part, cos_z) - to_last(real_part, sin_z)
    stacked = jnp.stack([spec_re, spec_im], axis=-3)
    return stacked.reshape(stacked.shape[:-2] + (MY * MZ,))


def forward_x(slab, normalize_scale):
    cos_x, sin_x = fourier_tables(NX, MX)
    real_part = slab[:, :, :, 0]
    imag_part = slab[:, :, :, 1]
    spec_re = jnp.einsum("bxcp,xm->bmcp", real_part, cos_x, precision=precise) + jnp.einsum(
        "bxcp,xm->bmcp", imag_part, sin_x, precision=precise
    )
    spec_im = jnp.einsum("bxcp,xm->bmcp", imag_part, cos_x, precision=precise) - jnp.einsum(
        "bxcp,xm->bmcp", real_part, sin_x, precision=precise
    )
    return jnp.stack([spec_re, spec_im], axis=3) * normalize_scale


def multiply(weights, spectrum):
    w_re = weights[:, :, 0]
    w_im = weights[:, :, 1]
    s_re = spectrum[:, :, :, 0]
    s_im = spectrum[:, :, :, 1]
    t_re = jnp.einsum("mpoc,bmcp->bmop", w_re, s_re, precision=precise) - jnp.einsum(
        "mpoc,bmcp->bmop", w_im, s_im, precision=precise
    )
    t_im = jnp.einsum("mpoc,bmcp->bmop", w_re, s_im, precision=precise) + jnp.einsum(
        "mpoc,bmcp->bmop", w_im, s_re, precision=precise
    )
    return jnp.stack([t_re, t_im], axis=3)


def inverse_x(modes):
    cos_x, sin_x = fourier_tables(NX, MX)
    t_re = modes[:, :, :, 0]
    t_im = modes[:, :, :, 1]
    out_re = jnp.einsum("bmop,xm->bxop", t_re, cos_x, precision=precise) - jnp.einsum(
        "bmop,xm->bxop", t_im, sin_x, precision=precise
    )
    output_imaginary = jnp.einsum("bmop,xm->bxop", t_im, cos_x, precision=precise) + jnp.einsum(
        "bmop,xm->bxop", t_re, sin_x, precision=precise
    )
    return jnp.stack([out_re, output_imaginary], axis=3)


def inverse_plane(wave, normalize_scale):
    reshaped_array = wave.reshape(wave.shape[:-1] + (MY, MZ))
    w_re = reshaped_array[..., 0, :, :]
    w_im = reshaped_array[..., 1, :, :]
    cos_z, sin_z = fourier_tables(NZ, MZ)
    q_re = from_last(w_re, cos_z) - from_last(w_im, sin_z)
    q_im = from_last(w_im, cos_z) + from_last(w_re, sin_z)
    rounded = jnp.stack([q_re, q_im], axis=-3).astype(jnp.bfloat16)
    cos_y, sin_y = fourier_tables(NY, MY)
    lookup_table_y = jnp.stack([cos_y.T, -sin_y.T]).astype(jnp.bfloat16)
    return (
        jnp.einsum(
            "...orkz,rky->...oyz", rounded, lookup_table_y, preferred_element_type=jnp.float32
        )
        * normalize_scale
    )


def mode_grads(grads, spectrum):
    g_re = grads[:, :, :, 0]
    g_im = grads[:, :, :, 1]
    s_re = spectrum[:, :, :, 0]
    s_im = spectrum[:, :, :, 1]
    d_re = jnp.einsum("bmop,bmcp->mpoc", g_re, s_re, precision=precise) + jnp.einsum(
        "bmop,bmcp->mpoc", g_im, s_im, precision=precise
    )
    d_im = jnp.einsum("bmop,bmcp->mpoc", g_im, s_re, precision=precise) - jnp.einsum(
        "bmop,bmcp->mpoc", g_re, s_im, precision=precise
    )
    return jnp.stack([d_re, d_im], axis=2)


def central(values, axis):
    return (jnp.roll(values, -1, axis) - jnp.roll(values, 1, axis)) * 0.5


def local(fields, targets, multipliers, local_weight, proj_weight, spectral_weight):
    normalize_scale = 1.0 / math.sqrt(NX * NY * NZ)
    batch_all = fields.shape[0] * lax.axis_size("rep")

    def to_modes(pencil):
        return forward_x(pencil, normalize_scale)

    slab = forward_plane(fields)
    spectrum = to_modes(lax.all_to_all(slab, "gx", split_axis=4, concat_axis=1, tiled=True))
    full_weights = lax.all_gather(spectral_weight, "rep", axis=0, tiled=True).astype(jnp.float32)
    product = multiply(full_weights, spectrum)
    grid_back = inverse_x(product)
    spectral_part = inverse_plane(
        lax.all_to_all(grid_back, "gx", split_axis=1, concat_axis=4, tiled=True), normalize_scale
    )
    preact = (
        jnp.einsum("bxcyz,co->bxoyz", fields, local_weight, preferred_element_type=jnp.float32)
        + spectral_part
    )
    hidden = jax.nn.gelu(preact).astype(jnp.bfloat16)
    velocity = jnp.einsum(
        "bxoyz,oj->bxjyz", hidden, proj_weight, preferred_element_type=jnp.float32
    )
    padded_vel = extended(velocity[:, :, 0].astype(jnp.bfloat16), (("gx", 1),), 1).astype(
        jnp.float32
    )
    slope_x = (padded_vel[:, 2:] - padded_vel[:, :-2]) * 0.5
    divergence = slope_x + central(velocity[:, :, 1], 2) + central(velocity[:, :, 2], 3)
    lam = multipliers.astype(jnp.float32) / 64.0
    penalty = lam + penalty_weight * divergence
    misfit = velocity - targets.astype(jnp.float32)
    loss_sum = (
        jnp.sum(misfit * misfit)
        + jnp.sum(lam * divergence)
        + 0.5 * penalty_weight * jnp.sum(divergence * divergence)
    )
    padded_pen = extended(as_sent(penalty), (("gx", 1),), 1).astype(penalty.dtype)
    pen_x = (padded_pen[:, 2:] - padded_pen[:, :-2]) * 0.5
    slopes = jnp.stack([pen_x, central(penalty, 2), central(penalty, 3)], axis=2)
    grad_vel = ((2.0 * misfit - slopes) / batch_all).astype(jnp.bfloat16)
    grad_hidden = jnp.einsum(
        "bxjyz,oj->bxoyz", grad_vel, proj_weight, preferred_element_type=jnp.float32
    )
    grad_pre = jax.vjp(jax.nn.gelu, preact)[1](grad_hidden)[0].astype(jnp.bfloat16)
    grad_w = jnp.einsum("bxcyz,bxoyz->co", fields, grad_pre, preferred_element_type=jnp.float32)
    grad_q = jnp.einsum("bxoyz,bxjyz->oj", hidden, grad_vel, preferred_element_type=jnp.float32)
    summed = lax.psum((grad_w, grad_q, loss_sum), ("gx", "rep"))
    grad_slab = forward_plane(grad_pre)
    grads = to_modes(lax.all_to_all(grad_slab, "gx", split_axis=4, concat_axis=1, tiled=True))
    grad_r = lax.psum_scatter(mode_grads(grads, spectrum), "rep", scatter_dimension=0, tiled=True)
    loss = (summed[2] / (batch_all * NX * NY * NZ)).reshape(1)
    return (penalty, grad_r, summed[0] * normalize_scale, summed[1] * normalize_scale, loss)


def solution(mesh):
    in_specs = (
        P(("grp", "rep"), "gx", None, None, None),
        P(("grp", "rep"), "gx", None, None, None),
        P(("grp", "rep"), "gx", None, None),
        P(),
        P(),
        P("rep", "gx", None, None, None),
    )
    out_specs = (
        P(("grp", "rep"), "gx", None, None),
        P(("grp", "rep"), "gx", None, None, None),
        P("grp", None),
        P("grp", None),
        P("grp"),
    )
    return jax.shard_map(local, mesh=mesh, in_specs=in_specs, out_specs=out_specs, check_vma=False)
```

profile of v0, /device:TPU:0, one launch (start us, length us, event | category | flops | bytes accessed | tf_op | source)
XLA Modules:
  0.0 581.3 jit_solution(13471330185405126092)
XLA Ops:
  7.3 7.0 %fusion.49 = f32[1,16,32,2,16,128]{5,4,2,1,3,0:T(8,128)S(1)} fusion(bf16[1,16,32,128,128]{4,3,2,1,0:T(8,128)(2,1)} %param.6, bf16[128,1,16]{0,2,1:T(8,128)(2,1)S(1)} %get-tuple-element.83, bf16[128,1,16]{0,2,1:T(8,128)(2,1)S(1)} %get-tuple-element.82), kind=kOutput, calls=%fused_computation.72 | convolution fusion | flops 536887296 | bytes 25174016 | tf_op jit(solution)/shard_map/...cyz,yrk->...crkz/dot_general | solution.py:64
  18.1 5.2 fusion.42
  23.3 5.3 fusion.60
  31.6 7.4 %fusion.59 = f32[16,32,16,16]{3,2,1,0:T(8,128)} fusion(f32[16,32,16,16]{3,2,1,0:T(8,128)} %fusion.42, f32[1,16,32,2,16,128]{5,4,2,1,3,0:T(8,128)} %copy-done.3, s32[16]{0:T(128)S(1)} %compare_select_fusion), kind=kOutput, calls=%fused_computation.82 | convolution fusion | flops 201486336 | bytes 8912960 | tf_op jit(solution)/shard_map/...kz,zm->...km/dot_general | solution.py:54
  39.0 4.5 copy.174
  50.2 4.8 reshape.905
  55.0 7.3 %all-to-all-start = ((f32[8,1,32768]{2,1,0:T(1,128)}), f32[8,1,32768]{2,1,0:T(1,128)S(1)}, u32[]{:S(2)}, u32[]{:S(2)}) async-start(f32[8,1,32768]{2,1,0:T(1,128)} %reshape.905), calls=%async_computation | async-start | bytes 2097152 | tf_op jit(solution)/shard_map/all_to_all | solution.py:160
  63.0 25.0 %all-to-all-done = f32[8,1,32768]{2,1,0:T(1,128)S(1)} async-done(((f32[8,1,32768]{2,1,0:T(1,128)}), f32[8,1,32768]{2,1,0:T(1,128)S(1)}, u32[]{:S(2)}, u32[]{:S(2)}) %all-to-all-start) | async-done | bytes 1048608 | tf_op jit(solution)/shard_map/all_to_all | solution.py:160
  95.2 6.0 %copy.177 = f32[1,16,32,2,8,32]{5,2,3,1,4,0:T(8,128)} copy(f32[1,16,32,2,8,32]{2,1,3,5,4,0:T(8,128)} %bitcast.388) | data formatting | bytes 2097152 | tf_op jit(solution)/shard_map/all_to_all | solution.py:160
  118.5 11.4 %fusion.28 = (f32[16,32,32]{2,1,0:T(8,128)S(1)}, f32[16,32,32]{2,1,0:T(8,128)S(1)}, f32[16,32,32]{2,1,0:T(8,128)S(1)}, f32[16,32,32]{2,1,0:T(8,128)S(1)}) fusion(f32[16,32,32]{2,1,0:T(8,128)S(1)} %copy.262, bf16[16,32,2,32,32]{4,3,2,1,0:T(8,128)(2,1)} %all-gather.2.cloned.1.call-done, f32[16,32,32]{2,1,0:T(8,128)S(1)} %copy.261), kind=kLoop, calls=%fused_computation.39 | loop fusion | flops 5177344 | bytes 2490368
  139.3 4.8 reshape.907
  147.9 25.8 %all-to-all-done.1 = f32[8,1,32768]{2,1,0:T(1,128)S(1)} async-done(((f32[8,1,32768]{2,1,0:T(1,128)}), f32[8,1,32768]{2,1,0:T(1,128)S(1)}, u32[]{:S(2)}, u32[]{:S(2)}) %all-to-all-start.1) | async-done | bytes 1048608 | tf_op jit(solution)/shard_map/all_to_all | solution.py:165
  180.3 5.8 copy.181
  194.2 6.9 %fusion.33 = f32[16,32,16,128]{3,2,1,0:T(8,128)} fusion(f32[1,16,32,1,16,16]{5,4,2,1,3,0:T(8,128)} %copy.255, s32[16]{0:T(128)S(1)} %compare_select_fusion), kind=kOutput, calls=%fused_computation.54 | convolution fusion | flops 201355264 | bytes 4718656 | tf_op jit(solution)/shard_map/...km,zm->...kz/dot_general | solution.py:58
  201.1 5.2 fusion.35
  209.3 6.2 %fusion.70 = bf16[16,32,1,16,128]{4,3,1,0,2:T(8,128)(2,1)S(1)} fusion(f32[16,32,16,128]{3,2,1,0:T(8,128)} %fusion.33, f32[1,16,32,1,16,16]{5,4,2,1,3,0:T(8,128)} %copy.254, s32[16]{0:T(128)S(1)} %compare_select_fusion), kind=kOutput, calls=%fused_computation.87 | convolution fusion | flops 203452416 | bytes 6815808 | tf_op jit(solution)/shard_map/...km,zm->...kz/dot_general | solution.py:58
  219.5 13.1 %convolution_bitcast_fusion = f32[128,16,32,128]{3,0,2,1:T(8,128)} fusion(bf16[16,32,1,16,128]{4,3,1,0,2:T(8,128)(2,1)S(1)} %fusion.70, bf16[16,32,1,16,128]{4,3,1,0,2:T(8,128)(2,1)S(1)} %fusion.67, bf16[1,16,128]{2,1,0:T(8,128)(2,1)S(1)} %get-tuple-element.81, bf16[1,16,128]{2,1,0:T(8,128)(2,1)S(1)} %get-tuple-element.80), kind=kOutput, calls=%fused_computation.32 | convolution fusion | flops 545275904 | bytes 37756928 | tf_op jit(solution)/shard_map/...orkz,rky->...oyz/dot_general | solution.py:127
  232.6 56.0 %multiply_convert_fusion = (bf16[1,16,32,128,128]{4,2,3,1,0:T(8,128)(2,1)}, f32[1,16,32,128,128]{4,2,3,1,0:T(8,128)}) fusion(f32[128,16,32,128]{3,0,2,1:T(8,128)} %convolution_bitcast_fusion, bf16[16,32,128,128]{3,2,1,0:T(8,128)(2,1)} %bitcast.392, bf16[32,32]{1,0:T(8,128)(2,1)S(1)} %copy-done), kind=kOutput, calls=%fused_computation.16 | convolution fusion | flops 629145600 | bytes 100665344 | tf_op jit(solution)/shard_map/bxcyz,co->bxoyz/dot_general | solution.py:168
  288.7 8.2 %fusion.14 = f32[16,128,128,3]{2,3,1,0:T(4,128)S(1)} fusion(bf16[1,16,32,128,128]{4,2,3,1,0:T(8,128)(2,1)} %get-tuple-element.84, bf16[32,3]{0,1:T(4,128)(2,1)S(1)} %copy-done.20), kind=kOutput, calls=%fused_computation.22 | convolution fusion | flops 50331648 | bytes 19923136 | tf_op jit(solution)/shard_map/bxoyz,oj->bxjyz/dot_general | solution.py:172
  309.3 4.8 collective-permute-start.3
  318.1 34.7 %fusion.19 = bf16[16,32,128,128]{3,1,2,0:T(8,128)(2,1)} fusion(f32[1,16,32,128,128]{4,2,3,1,0:T(8,128)} %get-tuple-element.85, bf16[16,3,128,128]{3,2,1,0:T(8,128)(2,1)S(1)} %fusion.73, bf16[32,3]{0,1:T(4,128)(2,1)S(1)} %copy-done.20), kind=kOutput, calls=%fused_computation.27 | convolution fusion | flops 218103808 | bytes 51904704 | tf_op jit(solution)/shard_map/bxjyz,oj->bxoyz/dot_general | solution.py:192
  352.8 13.5 %fusion.52 = f32[1,16,32,2,16,128]{5,4,2,1,3,0:T(8,128)S(1)} fusion(bf16[16,32,128,128]{3,1,2,0:T(8,128)(2,1)} %fusion.19, bf16[128,1,16]{0,2,1:T(8,128)(2,1)S(1)} %copy-done.19, bf16[128,1,16]{0,2,1:T(8,128)(2,1)S(1)} %copy-done.17), kind=kOutput, calls=%fused_computation.73 | convolution fusion | flops 536887296 | bytes 25174016 | tf_op jit(solution)/shard_map/...cyz,yrk->...crkz/dot_general | solution.py:64
  370.0 5.2 fusion.46
  375.2 5.3 fusion.58
  383.5 7.4 %fusion.57 = f32[16,32,16,16]{3,2,1,0:T(8,128)} fusion(f32[16,32,16,16]{3,2,1,0:T(8,128)} %fusion.46, f32[1,16,32,2,16,128]{5,4,2,1,3,0:T(8,128)} %copy-done.2, s32[16]{0:T(128)S(1)} %compare_select_fusion), kind=kOutput, calls=%fused_computation.80 | convolution fusion | flops 201486336 | bytes 8912960 | tf_op jit(solution)/shard_map/...kz,zm->...km/dot_general | solution.py:54
  405.6 28.5 %all_to_all.51 = f32[8,1,32768]{2,1,0:T(1,128)S(1)} all-to-all(f32[8,1,32768]{2,1,0:T(1,128)S(1)} %reshape.909), channel_id=1, replica_groups=mesh['grp'=2,'gx'=8,'rep'=2] {'gx'}, dimensions={0} | all-to-all | bytes 2097152 | tf_op jit(solution)/shard_map/all_to_all | solution.py:200
  440.7 5.8 %copy.203 = f32[1,16,32,2,8,32]{5,2,3,1,4,0:T(8,128)} copy(f32[1,16,32,2,8,32]{2,1,3,5,4,0:T(8,128)} %bitcast.391) | data formatting | bytes 2097152 | tf_op jit(solution)/shard_map/all_to_all | solution.py:200
  465.5 4.8 add_bitcast_fusion
  470.3 7.3 %pad_maximum_fusion = f32[16,32,2,32,32]{4,3,2,1,0:T(8,128)} fusion(f32[16,32,1,32,32]{4,3,2,1,0:T(8,128)S(1)} %get-tuple-element.55, f32[16,32,1,32,32]{4,3,2,1,0:T(8,128)S(1)} %get-tuple-element.54), kind=kLoop, calls=%fused_computation.17 | loop fusion | flops 1048576 | bytes 8388608 | tf_op jit(solution)/shard_map/stack | solution.py:145
  479.6 9.6 %fusion.83 = f32[32,3]{0,1:T(4,128)S(1)} fusion(bf16[16,3,128,128]{3,2,1,0:T(8,128)(2,1)S(1)} %copy-done.15, bf16[1,16,32,128,128]{4,2,3,1,0:T(8,128)(2,1)} %get-tuple-element.84), kind=kOutput, calls=%fused_computation.102 | convolution fusion | flops 50331648 | bytes 18350464 | tf_op jit(solution)/shard_map/bxoyz,bxjyz->oj/dot_general | solution.py:197
  489.3 24.4 %fusion.80 = f32[32,32]{0,1:T(8,128)S(1)} fusion(bf16[16,32,128,128]{3,1,2,0:T(8,128)(2,1)} %fusion.19, bf16[16,32,128,128]{3,2,1,0:T(8,128)(2,1)} %bitcast.393), kind=kOutput, calls=%fused_computation.101 | convolution fusion | flops 536870912 | bytes 33558528 | tf_op jit(solution)/shard_map/bxcyz,bxoyz->co/dot_general | solution.py:196
  513.6 57.6 %all-reduce = (f32[32,32]{0,1:T(8,128)S(1)}, f32[32,3]{0,1:T(4,128)S(1)}, f32[]{:T(128)}) all-reduce(f32[32,32]{0,1:T(8,128)S(1)} %fusion.80, f32[32,3]{0,1:T(4,128)S(1)} %fusion.83, f32[]{:T(128)S(6)} %add.198), channel_id=1, replica_groups=mesh['grp'=2,'gx'=8,'rep'=2] {'gx','rep'}, use_global_device_ids=true, to_apply=%region_1.2 | all-reduce | flops 1121 | bytes 8968 | tf_op jit(solution)/shard_map/psum | solution.py:198
  (136 shorter events, 138.0 us)
Async XLA Ops:
  7.2 225.4 %copy-start = (bf16[32,32]{1,0:T(8,128)(2,1)S(1)}, bf16[32,32]{1,0:T(8,128)(2,1)}, u32[]{:S(2)}) copy-start(bf16[32,32]{1,0:T(8,128)(2,1)} %param.9) | copy-start | bytes 6148
  7.3 7.1 %copy-start.16 = (bf16[128,1,16]{0,2,1:T(8,128)(2,1)}, bf16[128,1,16]{0,2,1:T(8,128)(2,1)S(1)}, u32[]{:S(2)}) copy-start(bf16[128,1,16]{0,2,1:T(8,128)(2,1)S(1)} %get-tuple-element.82) | copy-start | bytes 12292
  7.3 7.1 %copy-start.18 = (bf16[128,1,16]{0,2,1:T(8,128)(2,1)}, bf16[128,1,16]{0,2,1:T(8,128)(2,1)S(1)}, u32[]{:S(2)}) copy-start(bf16[128,1,16]{0,2,1:T(8,128)(2,1)S(1)} %get-tuple-element.83) | copy-start | bytes 12292
  14.4 8.9 %copy-start.3 = (f32[1,16,32,2,16,128]{5,4,2,1,3,0:T(8,128)}, f32[1,16,32,2,16,128]{5,4,2,1,3,0:T(8,128)S(1)}, u32[]{:S(2)}) copy-start(f32[1,16,32,2,16,128]{5,4,2,1,3,0:T(8,128)S(1)} %fusion.49) | copy-start | bytes 25165828
  55.0 33.0 %all-to-all-start = ((f32[8,1,32768]{2,1,0:T(1,128)}), f32[8,1,32768]{2,1,0:T(1,128)S(1)}, u32[]{:S(2)}, u32[]{:S(2)}) async-start(f32[8,1,32768]{2,1,0:T(1,128)} %reshape.905), calls=%async_computation | async-start | bytes 2097152 | tf_op jit(solution)/shard_map/all_to_all | solution.py:160
  62.3 56.2 %all-gather.2.cloned.1.call-start = ((), (), s32[]{:S(2)}) async-start(), calls=%async_computation.4 | async-start | bytes 12582912 | tf_op jit(solution)/shard_map/all_gather | solution.py:161
  118.3 11.6 %copy-start.10 = (f32[16,32,32]{2,1,0:T(8,128)}, f32[16,32,32]{2,1,0:T(8,128)S(1)}, u32[]{:S(2)}) copy-start(f32[16,32,32]{2,1,0:T(8,128)S(1)} %copy.261) | copy-start | bytes 196612
  118.5 11.5 %copy-start.12 = (f32[16,32,32]{2,1,0:T(8,128)}, f32[16,32,32]{2,1,0:T(8,128)S(1)}, u32[]{:S(2)}) copy-start(f32[16,32,32]{2,1,0:T(8,128)S(1)} %copy.262) | copy-start | bytes 196612
  144.2 29.5 %all-to-all-start.1 = ((f32[8,1,32768]{2,1,0:T(1,128)}), f32[8,1,32768]{2,1,0:T(1,128)S(1)}, u32[]{:S(2)}, u32[]{:S(2)}) async-start(f32[8,1,32768]{2,1,0:T(1,128)} %reshape.907), calls=%async_computation.1 | async-start | bytes 2097152 | tf_op jit(solution)/shard_map/all_to_all | solution.py:165
  147.7 425.4 %reduce-scatter.2.cloned.1.call-start = ((), (), s32[]{:S(2)}) async-start(), calls=%async_computation.5 | async-start | bytes 25165824 | tf_op jit(solution)/shard_map/reduce_scatter | solution.py:201
  194.2 6.9 %copy-start.6 = (f32[1,16,32,1,16,16]{5,4,2,1,3,0:T(8,128)S(1)}, f32[1,16,32,1,16,16]{5,4,2,1,3,0:T(8,128)}, u32[]{:S(2)}) copy-start(f32[1,16,32,1,16,16]{5,4,2,1,3,0:T(8,128)} %copy.255) | copy-start | bytes 1572868
  209.3 6.2 %copy-start.5 = (f32[1,16,32,1,16,16]{5,4,2,1,3,0:T(8,128)S(1)}, f32[1,16,32,1,16,16]{5,4,2,1,3,0:T(8,128)}, u32[]{:S(2)}) copy-start(f32[1,16,32,1,16,16]{5,4,2,1,3,0:T(8,128)} %copy.254) | copy-start | bytes 1572868
  209.3 6.2 %copy-start.7 = (f32[16,32,16,128]{3,2,1,0:T(8,128)S(1)}, f32[16,32,16,128]{3,2,1,0:T(8,128)}, u32[]{:S(2)}) copy-start(f32[16,32,16,128]{3,2,1,0:T(8,128)} %fusion.35) | copy-start | bytes 12582916
  232.6 56.0 %copy-start.20 = (bf16[32,3]{0,1:T(4,128)(2,1)S(1)}, bf16[32,3]{0,1:T(4,128)(2,1)}, u32[]{:S(2)}) copy-start(bf16[32,3]{0,1:T(4,128)(2,1)} %param.10) | copy-start | bytes 580
  288.6 8.2 %copy-start.8 = (bf16[1,16,3,128,128]{4,3,2,1,0:T(8,128)(2,1)S(1)}, bf16[1,16,3,128,128]{4,3,2,1,0:T(8,128)(2,1)}, u32[]{:S(2)}) copy-start(bf16[1,16,3,128,128]{4,3,2,1,0:T(8,128)(2,1)} %param.7) | copy-start | bytes 4718596
  298.9 7.2 %copy-start.9 = (s32[1,16,128,128]{3,2,1,0:T(8,128)S(1)}, s32[1,16,128,128]{3,2,1,0:T(8,128)}, u32[]{:S(2)}) copy-start(s32[1,16,128,128]{3,2,1,0:T(8,128)} %param.8) | copy-start | bytes 3145732
  299.3 6.7 %collective-permute-start = (bf16[1,1,128,128]{3,2,1,0:T(8,128)(2,1)S(1)}, bf16[1,1,128,128]{3,2,1,0:T(8,128)(2,1)S(1)}, u32[]{:S(2)}, u32[]{:S(2)}) collective-permute-start(bf16[1,1,128,128]{3,2,1,0:T(8,128)(2,1)S(1)} %get-tuple-element.76), channel_id=1, source_target_pairs={{0,2},{2,4},{4,6},{6,8},{8,10},{10,12},{12,14},{14,0},{1,3},{3,5},... | collective-permute-start | bytes 98312 | tf_op jit(solution)/shard_map/ppermute | solution.py:27
  300.8 5.2 collective-permute-start.1
  307.9 1.0 copy-start.4
  309.2 6.7 %collective-permute-start.2 = (bf16[1,1,128,128]{3,2,1,0:T(8,128)(2,1)S(1)}, bf16[1,1,128,128]{3,2,1,0:T(8,128)(2,1)S(1)}, u32[]{:S(2)}, u32[]{:S(2)}) collective-permute-start(bf16[1,1,128,128]{3,2,1,0:T(8,128)(2,1)S(1)} %get-tuple-element.74), channel_id=1, source_target_pairs={{0,2},{2,4},{4,6},{6,8},{8,10},{10,12},{12,14},{14,0},{1,3},{3,5},... | collective-permute-start | bytes 98312 | tf_op jit(solution)/shard_map/ppermute | solution.py:27
  309.3 6.6 %collective-permute-start.3 = (bf16[1,1,128,128]{3,2,1,0:T(8,128)(2,1)S(1)}, bf16[1,1,128,128]{3,2,1,0:T(8,128)(2,1)S(1)}, u32[]{:S(2)}, u32[]{:S(2)}) collective-permute-start(bf16[1,1,128,128]{3,2,1,0:T(8,128)(2,1)S(1)} %get-tuple-element.75), channel_id=1, source_target_pairs={{2,0},{4,2},{6,4},{8,6},{10,8},{12,10},{14,12},{0,14},{3,1},{5,3},... | collective-permute-start | bytes 98312 | tf_op jit(solution)/shard_map/ppermute | solution.py:28
  316.9 1.2 copy-start.14
  318.1 34.7 %copy-start.17 = (bf16[128,1,16]{0,2,1:T(8,128)(2,1)S(1)}, bf16[128,1,16]{0,2,1:T(8,128)(2,1)}, u32[]{:S(2)}) copy-start(bf16[128,1,16]{0,2,1:T(8,128)(2,1)} %copy-done.16) | copy-start | bytes 12292
  318.1 34.7 %copy-start.19 = (bf16[128,1,16]{0,2,1:T(8,128)(2,1)S(1)}, bf16[128,1,16]{0,2,1:T(8,128)(2,1)}, u32[]{:S(2)}) copy-start(bf16[128,1,16]{0,2,1:T(8,128)(2,1)} %copy-done.18) | copy-start | bytes 12292
  366.3 8.9 %copy-start.2 = (f32[1,16,32,2,16,128]{5,4,2,1,3,0:T(8,128)}, f32[1,16,32,2,16,128]{5,4,2,1,3,0:T(8,128)S(1)}, u32[]{:S(2)}) copy-start(f32[1,16,32,2,16,128]{5,4,2,1,3,0:T(8,128)S(1)} %fusion.52) | copy-start | bytes 25165828
  456.1 9.3 %copy-start.11 = (f32[16,32,32]{2,1,0:T(8,128)S(1)}, f32[16,32,32]{2,1,0:T(8,128)}, u32[]{:S(2)}) copy-start(f32[16,32,32]{2,1,0:T(8,128)} %copy-done.10) | copy-start | bytes 196612
  457.4 8.1 %copy-start.13 = (f32[16,32,32]{2,1,0:T(8,128)S(1)}, f32[16,32,32]{2,1,0:T(8,128)}, u32[]{:S(2)}) copy-start(f32[16,32,32]{2,1,0:T(8,128)} %copy-done.12) | copy-start | bytes 196612
  477.6 2.0 copy-start.15
  489.3 83.9 %copy-start.1 = (bf16[32,32]{1,0:T(8,128)(2,1)S(1)}, bf16[32,32]{1,0:T(8,128)(2,1)}, u32[]{:S(2)}) copy-start(bf16[32,32]{1,0:T(8,128)(2,1)} %param.9) | copy-start | bytes 6148
Sparse Core Ops, SparseCore 0:
  64.6 21.2 all-gather.1
  477.7 25.3 reduce-scatter.1
where the time goes:
time: 590 us; the launch traced here: 581 us
  matrix products  255 us (43%)
  local copies, waits for them, and re-layouts  103 us (17%)
  blocking collectives  86.1 us (15%)
  waiting for transfers between devices  54.2 us (9%)
  other arithmetic  43.9 us (7%)
  starting transfers between devices  20.5 us (3%)
  between operations  18.6 us (3%)
    psum x1, blocking collectives, local(): summed = lax.psum((grad_w, grad_q, loss_sum), ('gx', 'rep'))  57.6 us
    dot_general x1, matrix products, local(): jnp.einsum('bxcyz,co->bxoyz', fields, local_weight, preferred_element_typ...  56 us
    dot_general x8, matrix products, to_last(): return jnp.einsum('...kz,zm->...km', values, table, precision=precise)  43.1 us
    unnamed x58, local copies, waits for them, and re-layouts  41.4 us
    dot_general x1, matrix products, local(): jnp.einsum('bxjyz,oj->bxoyz', grad_vel, proj_weight, preferred_element_ty...  34.7 us
    all_to_all x1, blocking collectives, local(): lax.all_to_all(grad_slab, 'gx', split_axis=4, concat_axis=1, tiled=True)  28.5 us
    all_to_all x1, waiting for transfers between devices, local(): lax.all_to_all(grid_back, 'gx', split_axis=1, concat_axis=4, tiled=True)  25.8 us
    all_to_all x1, waiting for transfers between devices, local(): lax.all_to_all(slab, 'gx', split_axis=4, concat_axis=1, tiled=True)  25 us
  transfers between devices with their start and end apart: 8, of which 4 were waited for; matrix products, arithmetic and copies ran while one was open for 11% of the time, Pallas kernels for 0%

commit v1 on v0

v1 whole, which is shorter than its diff:
```python
import functools
import math

import jax
import jax.numpy as jnp
import ml_dtypes
import numpy as np
from jax import lax
from jax.experimental import pallas as pl
from jax.experimental.pallas import tpu as pltpu
from jax.sharding import PartitionSpec as P

MX = 16
MY = 16
MZ = 16
ROWS = 16

penalty_weight = 0.5
precise = lax.Precision.HIGHEST
bf16 = jnp.bfloat16
f32 = jnp.float32
ROOT = math.sqrt(2.0 / math.pi)


def fourier_tables(length, count):
    position = np.arange(count)
    modes = np.where(position < count // 2, position, position - count)
    phase = np.mod(np.arange(length)[:, None] * modes[None, :], length)
    angle = phase.astype(np.float32) * np.float32(2.0 * math.pi / length)
    return np.cos(angle), np.sin(angle)


def halves(table):
    high = table.astype(ml_dtypes.bfloat16)
    low = (table - high.astype(np.float32)).astype(ml_dtypes.bfloat16)
    return high, low


def split(value):
    high = value.astype(bf16)
    return high, (value - high.astype(f32)).astype(bf16)


def dot(a, b):
    return jnp.dot(a, b, preferred_element_type=f32)


def dot_nt(a, b):
    return lax.dot_general(a, b, (((1,), (1,)), ((), ())), preferred_element_type=f32)


def dot_tn(a, b):
    return lax.dot_general(a, b, (((0,), (0,)), ((), ())), preferred_element_type=f32)


def plane_modes(load, count, ty, zt):
    parts = jnp.stack([dot(ty, load(c)) for c in range(count)], axis=0)
    turned = jnp.swapaxes(parts, 0, 1)
    nz = turned.shape[-1]
    real = turned[:MY].reshape(MY * count, nz)
    imag = turned[MY:].reshape(MY * count, nz)
    high, low = split(jnp.concatenate([real, imag], axis=1))
    both = dot_nt(zt, high)
    n = 2 * MZ
    return both[:n] + both[n:] + dot_nt(zt[:n], low)


def forward_body(f_ref, ty_ref, zt_ref, out_ref):
    count = f_ref.shape[1]
    out_ref[0] = plane_modes(lambda c: f_ref[0, c], count, ty_ref[...], zt_ref[...])


def tile_pair(ref, y0):
    count, nz = ref.shape[1], ref.shape[3]
    one = ref[0, :, pl.ds(y0, ROWS), :].reshape(count * ROWS, nz)
    two = ref[0, :, pl.ds(y0 + ROWS, ROWS), :].reshape(count * ROWS, nz)
    return jnp.concatenate([one, two], axis=1)


def put_pair(ref, y0, value):
    count, nz = ref.shape[1], ref.shape[3]
    ref[0, :, pl.ds(y0, ROWS), :] = value[:, :nz].reshape(count, ROWS, nz)
    ref[0, :, pl.ds(y0 + ROWS, ROWS), :] = value[:, nz:].reshape(count, ROWS, nz)


def middle_body(scale, f_ref, m_ref, zi_ref, yi_ref, kw_ref, kp_ref, pre_ref, vel_ref):
    count, ny, nz = f_ref.shape[1], f_ref.shape[2], f_ref.shape[3]
    high, low = split(m_ref[0])
    wave = dot_tn(jnp.concatenate([high, high, low], axis=0), zi_ref[...])
    turned = jnp.swapaxes(wave.reshape(MY, count, 2 * nz), 0, 1)
    yi = yi_ref[...]
    for o in range(0, count, 2):
        pair = [
            jnp.concatenate([turned[i, :, :nz], turned[i, :, nz:]], axis=0) for i in (o, o + 1)
        ]
        both = dot(yi, jnp.concatenate(pair, axis=1).astype(bf16))
        pre_ref[0, o] = both[:, :nz] * scale
        pre_ref[0, o + 1] = both[:, nz:] * scale

    @pl.loop(0, ny // (2 * ROWS))
    def _(step):
        y0 = pl.multiple_of(step * 2 * ROWS, 2 * ROWS)
        x = tile_pair(pre_ref, y0) + dot(kw_ref[...], tile_pair(f_ref, y0))
        put_pair(pre_ref, y0, x)
        t = jnp.tanh(ROOT * (x + 0.044715 * (x * x * x)))
        hidden = (x * (0.5 * (1.0 + t))).astype(bf16)
        put_pair(vel_ref, y0, dot(kp_ref[...], hidden))


def backward_body(
    f_ref, pre_ref, gv_ref, ty_ref, zt_ref, kpt_ref, out_ref, gw_ref, gq_ref, gp_ref
):
    count, ny, nz = f_ref.shape[1], f_ref.shape[2], f_ref.shape[3]

    @pl.when(pl.program_id(0) == 0)
    def _():
        gw_ref[...] = jnp.zeros_like(gw_ref)
        gq_ref[...] = jnp.zeros_like(gq_ref)

    @pl.loop(0, ny // (2 * ROWS))
    def _(step):
        y0 = pl.multiple_of(step * 2 * ROWS, 2 * ROWS)
        gv = tile_pair(gv_ref, y0)
        x = tile_pair(pre_ref, y0)
        xx = x * x
        t = jnp.tanh(ROOT * (x + 0.044715 * (xx * x)))
        cdf = 0.5 * (1.0 + t)
        hidden = (x * cdf).astype(bf16)
        slope = cdf + x * (0.5 * (1.0 - t * t)) * (ROOT + (3.0 * 0.044715 * ROOT) * xx)
        gp = (dot(kpt_ref[...], gv) * slope).astype(bf16)
        put_pair(gp_ref, y0, gp)
        gw_ref[...] += dot_nt(tile_pair(f_ref, y0), gp)
        gq_ref[...] += dot_nt(hidden, gv)

    out_ref[0] = plane_modes(lambda c: gp_ref[0, c], count, ty_ref[...], zt_ref[...])


def whole(shape):
    return pl.BlockSpec(shape, lambda i: (0,) * len(shape))


def plane(shape):
    return pl.BlockSpec((1,) + tuple(shape), lambda i: (i,) + (0,) * len(shape))


params = pltpu.CompilerParams(
    dimension_semantics=("arbitrary",), vmem_limit_bytes=56 * 1024 * 1024
)


def extended(value, axis_name):
    count = lax.axis_size(axis_name)
    up = [(i, (i + 1) % count) for i in range(count)]
    down = [(j, i) for i, j in up]
    before = lax.ppermute(value[-1:], axis_name, up)
    after = lax.ppermute(value[:1], axis_name, down)
    return jnp.concatenate([before, value, after], axis=0)


def central(values, axis):
    return (jnp.roll(values, -1, axis) - jnp.roll(values, 1, axis)) * 0.5


def local(fields, targets, multipliers, local_weight, proj_weight, spectral_weight):
    gx = lax.axis_size("gx")
    rep = lax.axis_size("rep")
    _, xl, C, NY, NZ = fields.shape
    NX = xl * gx
    PL = MY * MZ // gx
    scale = 1.0 / math.sqrt(NX * NY * NZ)
    fields, targets, multipliers = fields[0], targets[0], multipliers[0]

    cos_y, sin_y = fourier_tables(NY, MY)
    ty = jnp.asarray(np.concatenate([cos_y.T, -sin_y.T], 0).astype(ml_dtypes.bfloat16))
    yi = jnp.asarray(np.concatenate([cos_y, -sin_y], 1).astype(ml_dtypes.bfloat16))
    cos_z, sin_z = fourier_tables(NZ, MZ)
    zt = np.concatenate(
        [np.concatenate([cos_z.T, sin_z.T], 1), np.concatenate([-sin_z.T, cos_z.T], 1)], 0
    )
    zt = jnp.asarray(np.concatenate(halves(zt), 0))
    zi = np.concatenate(
        [np.concatenate([cos_z.T, sin_z.T], 1), np.concatenate([-sin_z.T, cos_z.T], 1)], 0
    )
    zi_high, zi_low = halves(zi)
    zi = jnp.asarray(np.concatenate([zi_high, zi_low, zi_high], 0))
    cos_x, sin_x = fourier_tables(NX, MX)
    xt = np.stack(
        [np.stack([cos_x.T, sin_x.T], 1), np.stack([-sin_x.T, cos_x.T], 1)], 1
    )
    xt = xt.reshape(MX, 2, 2, gx, xl).transpose(0, 1, 3, 2, 4).reshape(2 * MX, 2 * NX)
    x_forward = jnp.asarray(xt * np.float32(scale))
    x_back = jnp.asarray(np.ascontiguousarray(xt.T))

    eye = jnp.eye(ROWS, dtype=bf16)
    kw = jnp.kron(local_weight.T, eye)
    kp = jnp.kron(proj_weight.T, eye)
    kpt = jnp.kron(proj_weight, eye)

    modes_shape = jax.ShapeDtypeStruct((xl, 2 * MZ, MY * C), f32)
    field_spec = plane((C, NY, NZ))
    modes_spec = plane((2 * MZ, MY * C))
    vel_spec = plane((3, NY, NZ))

    def to_owner(slab):
        slab = slab.reshape(xl, 2, MZ, MY, C).transpose(3, 2, 1, 0, 4)
        slab = slab.reshape(gx, PL, 2, xl, C).transpose(0, 2, 3, 1, 4)
        slab = slab.reshape(gx, 2 * xl, PL * C)
        slab = lax.all_to_all(slab, "gx", split_axis=0, concat_axis=0, tiled=True)
        out = jnp.dot(x_forward, slab.reshape(2 * NX, PL * C), precision=precise)
        return out.reshape(MX, 2, PL, C)

    def to_planes(modes):
        out = jnp.dot(x_back, modes.reshape(2 * MX, PL * C), precision=precise)
        out = out.reshape(gx, 2 * xl, PL * C)
        out = lax.all_to_all(out, "gx", split_axis=0, concat_axis=0, tiled=True)
        out = out.reshape(gx, 2, xl, PL, C).transpose(0, 3, 1, 2, 4)
        out = out.reshape(MY, MZ, 2, xl, C).transpose(3, 2, 1, 0, 4)
        return out.reshape(xl, 2 * MZ, MY * C)

    def both_samples(modes):
        part = modes.reshape(rep, MX // rep, 2, PL, C)
        return lax.all_to_all(part, "rep", split_axis=0, concat_axis=0, tiled=True)

    slab = pl.pallas_call(
        forward_body,
        grid=(xl,),
        out_shape=modes_shape,
        in_specs=[field_spec, whole(ty.shape), whole(zt.shape)],
        out_specs=modes_spec,
        compiler_params=params,
    )(fields, ty, zt)
    spectrum = to_owner(slab)
    weights = lax.all_gather(spectral_weight, "rep", axis=0, tiled=True).astype(f32)
    w_re, w_im = weights[:, :, 0], weights[:, :, 1]
    s_re, s_im = spectrum[:, 0], spectrum[:, 1]

    def apply(w, s):
        return jnp.einsum("mpoc,mpc->mpo", w, s, precision=precise)

    product = jnp.stack(
        [apply(w_re, s_re) - apply(w_im, s_im), apply(w_re, s_im) + apply(w_im, s_re)], axis=1
    )
    wave = to_planes(product)
    spectra = both_samples(spectrum)

    pre, velocity = pl.pallas_call(
        functools.partial(middle_body, scale),
        grid=(xl,),
        out_shape=(
            jax.ShapeDtypeStruct((xl, C, NY, NZ), f32),
            jax.ShapeDtypeStruct((xl, 3, NY, NZ), f32),
        ),
        in_specs=[
            field_spec,
            modes_spec,
            whole(zi.shape),
            whole(yi.shape),
            whole(kw.shape),
            whole(kp.shape),
        ],
        out_specs=(field_spec, vel_spec),
        compiler_params=params,
    )(fields, wave, zi, yi, kw, kp)

    padded = extended(velocity[:, 0].astype(bf16), "gx").astype(f32)
    slope_x = (padded[2:] - padded[:-2]) * 0.5
    divergence = slope_x + central(velocity[:, 1], 1) + central(velocity[:, 2], 2)
    lam = multipliers.astype(f32) / 64.0
    penalty = lam + penalty_weight * divergence
    misfit = velocity - targets.astype(f32)
    loss_sum = (
        jnp.sum(misfit * misfit)
        + jnp.sum(lam * divergence)
        + 0.5 * penalty_weight * jnp.sum(divergence * divergence)
    )
    padded = extended(penalty.astype(bf16), "gx").astype(f32)
    pen_x = (padded[2:] - padded[:-2]) * 0.5
    slopes = jnp.stack([pen_x, central(penalty, 1), central(penalty, 2)], axis=1)
    grad_vel = ((2.0 * misfit - slopes) / rep).astype(bf16)

    wide = C * ROWS
    grad_slab, gw, gq = pl.pallas_call(
        backward_body,
        grid=(xl,),
        out_shape=(
            modes_shape,
            jax.ShapeDtypeStruct((wide, wide), f32),
            jax.ShapeDtypeStruct((wide, 3 * ROWS), f32),
        ),
        in_specs=[
            field_spec,
            field_spec,
            vel_spec,
            whole(ty.shape),
            whole(zt.shape),
            whole(kpt.shape),
        ],
        out_specs=(modes_spec, whole((wide, wide)), whole((wide, 3 * ROWS))),
        scratch_shapes=[pltpu.VMEM((1, C, NY, NZ), bf16)],
        compiler_params=params,
    )(fields, pre, grad_vel, ty, zt, kpt)

    grads = both_samples(to_owner(grad_slab))

    gather = jnp.asarray(np.kron(np.eye(C), np.ones((1, ROWS))).astype(np.float32))
    gather_q = jnp.asarray(np.kron(np.eye(3), np.ones((ROWS, 1))).astype(np.float32))
    mask = jnp.asarray(np.kron(np.ones((C, C)), np.eye(ROWS)).astype(np.float32))
    mask_q = jnp.asarray(np.kron(np.ones((C, 3)), np.eye(ROWS)).astype(np.float32))
    grad_w = jnp.dot(jnp.dot(gather, gw * mask, precision=precise), gather.T, precision=precise)
    grad_q = jnp.dot(jnp.dot(gather, gq * mask_q, precision=precise), gather_q, precision=precise)
    packed = jnp.concatenate([grad_w.reshape(-1), grad_q.reshape(-1), loss_sum.reshape(1)])
    packed = lax.psum(packed, ("gx", "rep"))
    grad_w = packed[: C * C].reshape(C, C) * scale
    grad_q = packed[C * C : C * C + 3 * C].reshape(C, 3) * scale
    loss = packed[-1:] / (rep * NX * NY * NZ)

    g_re, g_im = grads[:, :, 0], grads[:, :, 1]
    s_re, s_im = spectra[:, :, 0], spectra[:, :, 1]

    def outer(g, s):
        return jnp.sum(g[..., :, None] * s[..., None, :], axis=0)

    grad_r = jnp.stack(
        [outer(g_re, s_re) + outer(g_im, s_im), outer(g_im, s_re) - outer(g_re, s_im)], axis=2
    )
    return (penalty[None], grad_r, grad_w, grad_q, loss)


def solution(mesh):
    in_specs = (
        P(("grp", "rep"), "gx", None, None, None),
        P(("grp", "rep"), "gx", None, None, None),
        P(("grp", "rep"), "gx", None, None),
        P(),
        P(),
        P("rep", "gx", None, None, None),
    )
    out_specs = (
        P(("grp", "rep"), "gx", None, None),
        P(("grp", "rep"), "gx", None, None, None),
        P("grp", None),
        P("grp", None),
        P("grp"),
    )
    return jax.shard_map(local, mesh=mesh, in_specs=in_specs, out_specs=out_specs, check_vma=False)
```

time: 590 us -> 413 us (0.70)
  matrix products: 255 us -> 36.2 us
  Pallas kernels: 0 us -> 125 us
  blocking collectives: 86.1 us -> 40.1 us
  local copies, waits for them, and re-layouts: 103 us -> 85.6 us
  other arithmetic: 43.9 us -> 29.6 us
  waiting for transfers between devices: 54.2 us -> 47.3 us
    dot_general x32 -> x11, matrix products: 255 us -> 36.2 us  [the longest x4 30 us: apply(): return jnp.einsum('mpoc,mpc->mpo', w, s, precision=precise)]
    pallas_call x0 -> x3, Pallas kernels: none -> 125 us  [the longest x1 57.3 us: local(): pl.pallas_call(backward_body, grid=(xl,), out_shape=(modes_shape, jax.Sha...]
    reshape x0 -> x12, local copies, waits for them, and re-layouts: none -> 42 us  [the longest x4 16.7 us: to_owner(): slab = slab.reshape(xl, 2, MZ, MY, C).transpose(3, 2, 1, 0, 4)]
    unnamed x58 -> x34, local copies, waits for them, and re-layouts: 41.4 us -> 8.17 us
    all_to_all x1, blocking collectives: 28.5 us -> 3.84 us  [both_samples(): return lax.all_to_all(part, 'rep', split_axis=0, concat_axis=0, tiled=True)]
    psum x1, blocking collectives: 57.6 us -> 36.2 us  [local(): packed = lax.psum(packed, ('gx', 'rep'))]
    transpose x0 -> x5, local copies, waits for them, and re-layouts: none -> 17.9 us  [the longest x2 8.78 us: to_owner(): slab = slab.reshape(gx, PL, 2, xl, C).transpose(0, 2, 3, 1, 4)]
    all_to_all x4 -> x1, local copies, waits for them, and re-layouts: 18.1 us -> 0.51 us  [both_samples(): return lax.all_to_all(part, 'rep', split_axis=0, concat_axis=0, tiled=True)]
  transfers between devices with their start and end apart: 8 -> 9, of which waited for: 4 -> 6; matrix products, arithmetic and copies ran while one was open for 11% -> 18% of each run, Pallas kernels for 0% -> 27%
where the time goes in v1:
time: 413 us; the launch traced here: 405 us
  Pallas kernels  125 us (30%)
  local copies, waits for them, and re-layouts  85.6 us (21%)
  waiting for transfers between devices  47.3 us (11%)
  blocking collectives  40.1 us (10%)
  matrix products  36.2 us (9%)
  other arithmetic  29.6 us (7%)
  starting transfers between devices  23.2 us (6%)
  between operations  18.7 us (5%)
    pallas_call x1, Pallas kernels, local(): pl.pallas_call(backward_body, grid=(xl,), out_shape=(modes_shape, jax.Sha...  57.3 us
    pallas_call x1, Pallas kernels, local(): pl.pallas_call(functools.partial(middle_body, scale), grid=(xl,), out_sha...  50.3 us
    psum x1, blocking collectives, local(): packed = lax.psum(packed, ('gx', 'rep'))  36.2 us
    dot_general x4, matrix products, apply(): return jnp.einsum('mpoc,mpc->mpo', w, s, precision=precise)  30 us
    all_to_all x2, waiting for transfers between devices, to_owner(): slab = lax.all_to_all(slab, 'gx', split_axis=0, concat_axis=0, tiled=True)  25 us
    pallas_call x1, Pallas kernels, local(): pl.pallas_call(forward_body, grid=(xl,), out_shape=modes_shape, in_specs=...  17.3 us
    reshape x4, local copies, waits for them, and re-layouts, to_owner(): slab = slab.reshape(xl, 2, MZ, MY, C).transpose(3, 2, 1, 0, 4)  16.7 us
    reduce_sum x1, other arithmetic, outer(): return jnp.sum(g[..., :, None] * s[..., None, :], axis=0)  12.1 us
  transfers between devices with their start and end apart: 9, of which 6 were waited for; matrix products, arithmetic and copies ran while one was open for 18% of the time, Pallas kernels for 27%

profile of v1, /device:TPU:0, one launch (start us, length us, event | category | flops | bytes accessed | tf_op | source)
XLA Modules:
  0.0 405.5 jit_solution(15495734903445202850)
XLA Ops:
  7.2 17.3 %shard_map.191 = f32[16,32,512]{2,1,0:T(8,128)} custom-call(bf16[16,32,128,128]{3,2,1,0:T(8,128)(2,1)} %bitcast.148, bf16[32,128]{1,0:T(8,128)(2,1)} %constant.39.clone.ty_ref, bf16[64,256]{1,0:T(8,128)(2,1)} %constant.41.clone.zt_ref), custom_call_target="tpu_custom_call" | custom-call | tf_op jit(solution)/shard_map/pallas_call | solution.py:224
  24.4 3.7 reshape.245
  28.2 4.6 %copy.96 = f32[16,2,16,16,32]{4,0,1,2,3:T(8,128)S(1)} copy(f32[16,2,16,16,32]{4,3,2,1,0:T(8,128)} %reshape.245) | data formatting | bytes 2097152 | tf_op jit(solution)/shard_map/reshape | solution.py:205
  32.8 4.4 %copy.97 = f32[8,2,16,32,32]{4,3,2,1,0:T(8,128)} copy(f32[8,2,16,32,32]{4,2,1,3,0:T(8,128)S(1)} %bitcast.153) | data formatting | bytes 2097152 | tf_op jit(solution)/shard_map/transpose | solution.py:206
  37.2 4.6 %reshape.247 = f32[8,32,1024]{2,1,0:T(8,128)} reshape(f32[8,2,16,32,32]{4,3,2,1,0:T(8,128)} %copy.97) | data formatting | bytes 2097152 | tf_op jit(solution)/shard_map/reshape | solution.py:207
  41.8 7.4 %all-to-all-start = ((f32[8,32,1024]{2,1,0:T(8,128)}), f32[8,32,1024]{2,1,0:T(8,128)S(1)}, u32[]{:S(2)}, u32[]{:S(2)}) async-start(f32[8,32,1024]{2,1,0:T(8,128)} %reshape.247), calls=%async_computation | async-start | bytes 2097152 | tf_op jit(solution)/shard_map/all_to_all | solution.py:208
  49.9 25.0 %all-to-all-done = f32[8,32,1024]{2,1,0:T(8,128)S(1)} async-done(((f32[8,32,1024]{2,1,0:T(8,128)}), f32[8,32,1024]{2,1,0:T(8,128)S(1)}, u32[]{:S(2)}, u32[]{:S(2)}) %all-to-all-start) | async-done | bytes 1048608 | tf_op jit(solution)/shard_map/all_to_all | solution.py:208
  75.9 8.5 %fusion.2 = f32[16,32,1,32]{3,2,1,0:T(1,128)S(1)} fusion(f32[16,32,32,1]{2,3,1,0:T(1,128)S(1)} %bitcast.162, bf16[16,32,2,32,32]{4,3,2,1,0:T(8,128)(2,1)} %all-gather.2.cloned.1.call-done), kind=kOutput, calls=%fused_computation.11 | convolution fusion | flops 6291456 | bytes 4325376 | tf_op jit(solution)/shard_map/mpoc,mpc->mpo/dot_general | solution.py:238
  84.4 8.3 %fusion.1 = f32[16,32,1,32]{3,2,1,0:T(1,128)S(1)} fusion(f32[16,32,32,1]{2,3,1,0:T(1,128)S(1)} %bitcast.163, bf16[16,32,2,32,32]{4,3,2,1,0:T(8,128)(2,1)} %all-gather.2.cloned.1.call-done), kind=kOutput, calls=%fused_computation.10 | convolution fusion | flops 6291456 | bytes 4325376 | tf_op jit(solution)/shard_map/mpoc,mpc->mpo/dot_general | solution.py:238
  92.7 6.6 %fusion = f32[16,32,1,32]{3,2,1,0:T(1,128)S(1)} fusion(f32[16,32,32,1]{2,3,1,0:T(1,128)S(1)} %bitcast.158, bf16[16,32,2,32,32]{4,3,2,1,0:T(8,128)(2,1)S(1)} %copy-done.13), kind=kOutput, calls=%fused_computation.9 | convolution fusion | flops 6291456 | bytes 4521984 | tf_op jit(solution)/shard_map/mpoc,mpc->mpo/dot_general | solution.py:238
  99.3 6.6 %fusion.3 = f32[16,32,1,32]{3,2,1,0:T(1,128)S(1)} fusion(f32[16,32,32,1]{2,3,1,0:T(1,128)S(1)} %bitcast.159, bf16[16,32,2,32,32]{4,3,2,1,0:T(8,128)(2,1)S(1)} %copy-done.13), kind=kOutput, calls=%fused_computation.12 | convolution fusion | flops 6291456 | bytes 4521984 | tf_op jit(solution)/shard_map/mpoc,mpc->mpo/dot_general | solution.py:238
  108.2 3.6 all-to-all-start.1
  114.4 8.4 %mul.196.kw_ref = bf16[512,512]{1,0:T(8,128)(2,1)} reshape(bf16[32,16,32,16]{3,2,1,0:T(8,128)(2,1)} %broadcast_multiply_fusion) | data formatting | bytes 1048576 | tf_op jit(solution)/shard_map/jit(kron)/mul | solution.py:195
  126.4 11.4 %all-to-all-done.1 = f32[8,32,1024]{2,1,0:T(8,128)S(1)} async-done(((f32[8,32,1024]{2,1,0:T(8,128)}), f32[8,32,1024]{2,1,0:T(8,128)S(1)}, u32[]{:S(2)}, u32[]{:S(2)}) %all-to-all-start.1) | async-done | bytes 1048608 | tf_op jit(solution)/shard_map/all_to_all | solution.py:215
  137.8 3.4 all-to-all-start.4
  141.1 11.1 %reshape.252 = f32[8,2,16,32,32]{4,3,2,1,0:T(8,128)} reshape(f32[8,32,1024]{2,1,0:T(8,128)S(1)} %all-to-all-done.1) | data formatting | bytes 2097152 | tf_op jit(solution)/shard_map/reshape | solution.py:216
  152.3 4.6 %copy.98 = f32[8,32,2,16,32]{4,3,2,1,0:T(8,128)S(1)} copy(f32[8,32,2,16,32]{4,1,3,2,0:T(8,128)} %bitcast.152) | data formatting | bytes 2097152 | tf_op jit(solution)/shard_map/transpose | solution.py:216
  156.8 4.4 %copy.99 = f32[16,2,16,16,32]{4,3,2,1,0:T(8,128)} copy(f32[16,2,16,16,32]{4,0,1,2,3:T(8,128)S(1)} %bitcast.154) | data formatting | bytes 2097152 | tf_op jit(solution)/shard_map/transpose | solution.py:217
  161.3 4.4 %reshape.254.m_ref = f32[16,32,512]{2,1,0:T(8,128)} reshape(f32[16,2,16,16,32]{4,3,2,1,0:T(8,128)} %copy.99) | data formatting | bytes 2097152 | tf_op jit(solution)/shard_map/reshape | solution.py:218
  165.7 50.3 %shard_map.192 = (f32[16,32,128,128]{3,2,1,0:T(8,128)}, f32[16,3,128,128]{3,2,1,0:T(8,128)}) custom-call(bf16[16,32,128,128]{3,2,1,0:T(8,128)(2,1)} %bitcast.149, f32[16,32,512]{2,1,0:T(8,128)} %reshape.254.m_ref, bf16[96,256]{1,0:T(8,128)(2,1)} %constant.42.clone.zi_ref, bf16[128,32]{1,0:T(8,128)(2,1)} %constant.40.clone.yi_ref, ...), custom_call_target="tpu_custom_call" | custom-call | tf_op jit(solution)/shard_map/pallas_call | solution.py:246
  224.0 5.0 %collective-permute-done = bf16[1,128,128]{2,1,0:T(8,128)(2,1)S(1)} collective-permute-done((bf16[1,128,128]{2,1,0:T(8,128)(2,1)S(1)}, bf16[1,128,128]{2,1,0:T(8,128)(2,1)S(1)}, u32[]{:S(2)}, u32[]{:S(2)}) %collective-permute-start) | collective-permute-done | bytes 32800 | tf_op jit(solution)/shard_map/ppermute | solution.py:155
  241.9 57.3 %shard_map.193 = (f32[16,32,512]{2,1,0:T(8,128)}, f32[512,512]{1,0:T(8,128)}, f32[512,48]{1,0:T(8,128)}) custom-call(bf16[16,32,128,128]{3,2,1,0:T(8,128)(2,1)} %bitcast.150, f32[16,32,128,128]{3,2,1,0:T(8,128)} %get-tuple-element.11.pre_ref, bf16[16,3,128,128]{3,2,1,0:T(8,128)(2,1)} %get-tuple-element.50.gv_ref, bf16[32,128]{1,0:T(8,128)(2,1)} %constant.39.clone.ty_ref, ...), custom_call_target="tpu_custom_call" | custom-call | tf_op jit(solution)/shard_map/pallas_call | solution.py:282
  299.2 3.7 reshape.255
  302.9 4.6 %copy.113 = f32[16,2,16,16,32]{4,0,1,2,3:T(8,128)S(1)} copy(f32[16,2,16,16,32]{4,3,2,1,0:T(8,128)} %reshape.255) | data formatting | bytes 2097152 | tf_op jit(solution)/shard_map/reshape | solution.py:205
  307.5 4.4 %copy.114 = f32[8,2,16,32,32]{4,3,2,1,0:T(8,128)} copy(f32[8,2,16,32,32]{4,2,1,3,0:T(8,128)S(1)} %bitcast.155) | data formatting | bytes 2097152 | tf_op jit(solution)/shard_map/transpose | solution.py:206
  311.9 4.6 %reshape.257 = f32[8,32,1024]{2,1,0:T(8,128)} reshape(f32[8,2,16,32,32]{4,3,2,1,0:T(8,128)} %copy.114) | data formatting | bytes 2097152 | tf_op jit(solution)/shard_map/reshape | solution.py:207
  316.5 4.0 all-to-all-start.2
  327.5 36.2 %psum.7 = f32[1121]{0:T(1024)S(1)} all-reduce(f32[1121]{0:T(1024)S(1)} %concatenate.99), channel_id=1, replica_groups=mesh['grp'=2,'gx'=8,'rep'=2] {'gx','rep'}, use_global_device_ids=true, to_apply=%region_7.8 | all-reduce | flops 1121 | bytes 8968 | tf_op jit(solution)/shard_map/psum | solution.py:312
  367.6 3.8 all_to_all.25
  373.4 12.1 %multiply_reduce_fusion.2 = (f32[8,32,32,32]{3,2,1,0:T(8,128)S(1)}, f32[8,32,32,32]{3,2,1,0:T(8,128)}, f32[8,32,32,32]{3,2,1,0:T(8,128)}, f32[8,32,32,32]{3,2,1,0:T(8,128)}) fusion(f32[2,8,32,32]{3,2,1,0:T(8,128)S(1)} %get-tuple-element.74, f32[2,8,32,32]{3,2,1,0:T(8,128)} %get-tuple-element.72, f32[2,8,32,32]{3,2,1,0:T(8,128)S(1)} %get-tuple-element.73, ...), kind=kLoop, calls=%fused_computation.3 | loop fusion | flops 3145728 | bytes 4456448 | tf_op jit(solution)/shard_map/reduce_sum | solution.py:321
  385.5 4.6 %subtract_bitcast_fusion = f32[8,32,1,32,32]{4,3,1,0,2:T(8,128)S(1)} fusion(f32[8,32,32,32]{3,2,1,0:T(8,128)} %get-tuple-element.43, f32[8,32,32,32]{3,2,1,0:T(8,128)} %get-tuple-element.45), kind=kLoop, calls=%fused_computation.7 | loop fusion | flops 262144 | bytes 3145728 | tf_op jit(solution)/shard_map/sub | solution.py:324
  392.6 4.4 %copy.116 = f32[8,32,2,32,32]{4,3,2,1,0:T(8,128)} copy(f32[8,32,2,32,32]{4,3,1,0,2:T(8,128)S(1)} %pad_maximum_fusion) | data formatting | bytes 4194304
  (104 shorter events, 43.5 us)
Async XLA Ops:
  41.8 33.2 %copy-start.9 = (f32[32,256]{1,0:T(8,128)S(1)}, f32[32,256]{1,0:T(8,128)}, u32[]{:S(2)}) copy-start(f32[32,256]{1,0:T(8,128)} %constant.43.clone) | copy-start | bytes 98308
  41.8 33.2 %all-to-all-start = ((f32[8,32,1024]{2,1,0:T(8,128)}), f32[8,32,1024]{2,1,0:T(8,128)S(1)}, u32[]{:S(2)}, u32[]{:S(2)}) async-start(f32[8,32,1024]{2,1,0:T(8,128)} %reshape.247), calls=%async_computation | async-start | bytes 2097152 | tf_op jit(solution)/shard_map/all_to_all | solution.py:208
  49.1 26.7 %all-gather.2.cloned.1.call-start = ((), (), s32[]{:S(2)}) async-start(), calls=%async_computation.5 | async-start | bytes 12582912 | tf_op jit(solution)/shard_map/all_gather | solution.py:233
  75.9 16.8 %copy-start.13 = (bf16[16,32,2,32,32]{4,3,2,1,0:T(8,128)(2,1)S(1)}, bf16[16,32,2,32,32]{4,3,2,1,0:T(8,128)(2,1)}, u32[]{:S(2)}) copy-start(bf16[16,32,2,32,32]{4,3,2,1,0:T(8,128)(2,1)} %all-gather.2.cloned.1.call-done) | copy-start | bytes 6291460
  99.3 7.0 %copy-start.8 = (f32[256,32]{1,0:T(8,128)S(1)}, f32[256,32]{1,0:T(8,128)}, u32[]{:S(2)}) copy-start(f32[256,32]{1,0:T(8,128)} %constant.44.clone) | copy-start | bytes 98308
  105.9 6.0 %copy-start.11 = (bf16[32,32]{1,0:T(8,128)(2,1)S(1)}, bf16[32,32]{1,0:T(8,128)(2,1)}, u32[]{:S(2)}) copy-start(bf16[32,32]{1,0:T(8,128)(2,1)} %param.19) | copy-start | bytes 6148
  108.2 29.5 %all-to-all-start.1 = ((f32[8,32,1024]{2,1,0:T(8,128)}), f32[8,32,1024]{2,1,0:T(8,128)S(1)}, u32[]{:S(2)}, u32[]{:S(2)}) async-start(f32[8,32,1024]{2,1,0:T(8,128)} %bitcast.26), calls=%async_computation.1 | async-start | bytes 2097152 | tf_op jit(solution)/shard_map/all_to_all | solution.py:215
  112.0 10.8 %copy-start.12 = (bf16[32,3]{0,1:T(4,128)(2,1)S(1)}, bf16[32,3]{0,1:T(4,128)(2,1)}, u32[]{:S(2)}) copy-start(bf16[32,3]{0,1:T(4,128)(2,1)} %param.20) | copy-start | bytes 580
  137.8 178.8 %all-to-all-start.4 = ((f32[2,1,16384]{2,1,0:T(1,128)}), f32[2,1,16384]{2,1,0:T(1,128)S(1)}, u32[]{:S(2)}, u32[]{:S(2)}) async-start(f32[2,1,16384]{2,1,0:T(1,128)} %reshape.269), calls=%async_computation.4 | async-start | bytes 262144 | tf_op jit(solution)/shard_map/all_to_all | solution.py:222
  217.6 1.9 copy-start.1
  219.8 9.4 %copy-start.3 = (s32[1,16,128,128]{3,2,1,0:T(8,128)S(1)}, s32[1,16,128,128]{3,2,1,0:T(8,128)}, u32[]{:S(2)}) copy-start(s32[1,16,128,128]{3,2,1,0:T(8,128)} %param.18) | copy-start | bytes 3145732
  220.1 4.0 collective-permute-start.1
  222.4 6.6 %collective-permute-start = (bf16[1,128,128]{2,1,0:T(8,128)(2,1)S(1)}, bf16[1,128,128]{2,1,0:T(8,128)(2,1)S(1)}, u32[]{:S(2)}, u32[]{:S(2)}) collective-permute-start(bf16[1,128,128]{2,1,0:T(8,128)(2,1)S(1)} %get-tuple-element.53), channel_id=1, source_target_pairs={{0,2},{2,4},{4,6},{6,8},{8,10},{10,12},{12,14},{14,0},{1,3},{3,5},... | collective-permute-start | bytes 98312 | tf_op jit(solution)/shard_map/ppermute | solution.py:155
  230.9 1.0 copy-start
  232.1 4.0 collective-permute-start.3
  232.1 6.9 %collective-permute-start.2 = (bf16[1,128,128]{2,1,0:T(8,128)(2,1)S(1)}, bf16[1,128,128]{2,1,0:T(8,128)(2,1)S(1)}, u32[]{:S(2)}, u32[]{:S(2)}) collective-permute-start(bf16[1,128,128]{2,1,0:T(8,128)(2,1)S(1)} %get-tuple-element.75), channel_id=1, source_target_pairs={{0,2},{2,4},{4,6},{6,8},{8,10},{10,12},{12,14},{14,0},{1,3},{3,5},... | collective-permute-start | bytes 98312 | tf_op jit(solution)/shard_map/ppermute | solution.py:155
  235.0 4.3 %copy-start.4 = (bf16[1,16,3,128,128]{4,3,2,1,0:T(8,128)(2,1)S(1)}, bf16[1,16,3,128,128]{4,3,2,1,0:T(8,128)(2,1)}, u32[]{:S(2)}) copy-start(bf16[1,16,3,128,128]{4,3,2,1,0:T(8,128)(2,1)} %param.17) | copy-start | bytes 4718596
  311.9 11.1 %copy-start.5 = (f32[32,512]{1,0:T(8,128)S(1)}, f32[32,512]{1,0:T(8,128)}, u32[]{:S(2)}) copy-start(f32[32,512]{1,0:T(8,128)} %constant.45.clone) | copy-start | bytes 196612
  316.5 9.0 %copy-start.6 = (f32[512,48]{1,0:T(8,128)S(1)}, f32[512,48]{1,0:T(8,128)}, u32[]{:S(2)}) copy-start(f32[512,48]{1,0:T(8,128)} %constant.48.clone) | copy-start | bytes 294916
  316.5 9.0 %copy-start.7 = (f32[512,48]{1,0:T(8,128)S(1)}, f32[512,48]{1,0:T(8,128)}, u32[]{:S(2)}) copy-start(f32[512,48]{1,0:T(8,128)} %get-tuple-element.14) | copy-start | bytes 294916
  316.5 9.3 %copy-start.10 = (f32[48,3]{1,0:T(8,128)S(1)}, f32[48,3]{1,0:T(8,128)}, u32[]{:S(2)}) copy-start(f32[48,3]{1,0:T(8,128)} %constant.46.clone) | copy-start | bytes 1732
  316.5 49.9 %all-to-all-start.2 = ((f32[8,32,1024]{2,1,0:T(8,128)}), f32[8,32,1024]{2,1,0:T(8,128)S(1)}, u32[]{:S(2)}, u32[]{:S(2)}) async-start(f32[8,32,1024]{2,1,0:T(8,128)} %reshape.257), calls=%async_computation.2 | async-start | bytes 2097152 | tf_op jit(solution)/shard_map/all_to_all | solution.py:208
  385.5 4.7 %copy-start.2 = (f32[8,32,32,32]{3,2,1,0:T(8,128)S(1)}, f32[8,32,32,32]{3,2,1,0:T(8,128)}, u32[]{:S(2)}) copy-start(f32[8,32,32,32]{3,2,1,0:T(8,128)} %get-tuple-element.44) | copy-start | bytes 3145732
Sparse Core Ops, SparseCore 0:
  51.5 21.2 all-gather.1

commit v2 on v1

--- a/solution.py
+++ b/solution.py
@@ -65,9 +65,57 @@
     return both[:n] + both[n:] + dot_nt(zt[:n], low)
 
 
+def store_modes(out_ref, modes):
+    if len(out_ref.shape) == 3:
+        out_ref[0] = modes
+        return
+    owners, _, _, high, lanes = out_ref.shape
+    width = modes.shape[1] // owners
+    rows = 2 * high
+    for d in range(owners):
+        parts = [
+            modes[j * rows : (j + 1) * rows, d * width : (d + 1) * width]
+            for j in range(lanes // width)
+        ]
+        out_ref[d, 0] = jnp.concatenate(parts, axis=1).reshape(2, high, lanes)
+
+
+def load_modes(m_ref, columns):
+    if len(m_ref.shape) == 3:
+        return m_ref[0]
+    owners, _, _, high, lanes = m_ref.shape
+    width = columns // owners
+    blocks = [m_ref[d, 0].reshape(2 * high, lanes) for d in range(owners)]
+    rows = [
+        jnp.concatenate([block[:, j * width : (j + 1) * width] for block in blocks], axis=1)
+        for j in range(lanes // width)
+    ]
+    return jnp.concatenate(rows, axis=0)
+
+
+def x_forward_body(slab_ref, table_ref, out_ref):
+    count = out_ref.shape[0]
+    xl = table_ref.shape[1] // (2 * slab_ref.shape[0])
+    value = slab_ref[:, :xl].reshape(table_ref.shape[1], count, out_ref.shape[2])
+    turned = jnp.swapaxes(value, 0, 1)
+    for k in range(count):
+        out_ref[k] = jnp.dot(
+            table_ref[...], turned[k], precision=precise, preferred_element_type=f32
+        )
+
+
+def x_back_body(modes_ref, table_ref, out_ref):
+    parts = [
+        jnp.dot(table_ref[...], modes_ref[k], precision=precise, preferred_element_type=f32)
+        for k in range(modes_ref.shape[0])
+    ]
+    turned = jnp.swapaxes(jnp.stack(parts, axis=0), 0, 1)
+    out_ref[...] = turned.reshape(out_ref.shape)
+
+
 def forward_body(f_ref, ty_ref, zt_ref, out_ref):
     count = f_ref.shape[1]
-    out_ref[0] = plane_modes(lambda c: f_ref[0, c], count, ty_ref[...], zt_ref[...])
+    store_modes(out_ref, plane_modes(lambda c: f_ref[0, c], count, ty_ref[...], zt_ref[...]))
 
 
 def tile_pair(ref, y0):
@@ -85,7 +133,7 @@
 
 def middle_body(scale, f_ref, m_ref, zi_ref, yi_ref, kw_ref, kp_ref, pre_ref, vel_ref):
     count, ny, nz = f_ref.shape[1], f_ref.shape[2], f_ref.shape[3]
-    high, low = split(m_ref[0])
+    high, low = split(load_modes(m_ref, MY * count))
     wave = dot_tn(jnp.concatenate([high, high, low], axis=0), zi_ref[...])
     turned = jnp.swapaxes(wave.reshape(MY, count, 2 * nz), 0, 1)
     yi = yi_ref[...]
@@ -132,7 +180,7 @@
         gw_ref[...] += dot_nt(tile_pair(f_ref, y0), gp)
         gq_ref[...] += dot_nt(hidden, gv)
 
-    out_ref[0] = plane_modes(lambda c: gp_ref[0, c], count, ty_ref[...], zt_ref[...])
+    store_modes(out_ref, plane_modes(lambda c: gp_ref[0, c], count, ty_ref[...], zt_ref[...]))
 
 
 def whole(shape):
@@ -177,17 +225,21 @@
     zt = np.concatenate(
         [np.concatenate([cos_z.T, sin_z.T], 1), np.concatenate([-sin_z.T, cos_z.T], 1)], 0
     )
-    zt = jnp.asarray(np.concatenate(halves(zt), 0))
-    zi = np.concatenate(
-        [np.concatenate([cos_z.T, sin_z.T], 1), np.concatenate([-sin_z.T, cos_z.T], 1)], 0
-    )
-    zi_high, zi_low = halves(zi)
+    direct = MY % gx == 0 and 128 % (MY // gx * C) == 0
+    KY = MY // gx if direct else 0
+    PK = 128 // (KY * C) if direct else 1
+    HZ = MZ // PK
+    order = np.arange(2 * MZ).reshape(2, HZ, PK).transpose(2, 0, 1).reshape(-1)
+    zt = zt[order]
+    zi_high, zi_low = halves(zt)
+    zt = jnp.asarray(np.concatenate([zi_high, zi_low], 0))
     zi = jnp.asarray(np.concatenate([zi_high, zi_low, zi_high], 0))
     cos_x, sin_x = fourier_tables(NX, MX)
     xt = np.stack(
         [np.stack([cos_x.T, sin_x.T], 1), np.stack([-sin_x.T, cos_x.T], 1)], 1
     )
-    xt = xt.reshape(MX, 2, 2, gx, xl).transpose(0, 1, 3, 2, 4).reshape(2 * MX, 2 * NX)
+    xt = xt.reshape(MX, 2, 2, gx, xl).transpose((0, 1, 3, 4, 2) if direct else (0, 1, 3, 2, 4))
+    xt = xt.reshape(2 * MX, 2 * NX)
     x_forward = jnp.asarray(xt * np.float32(scale))
     x_back = jnp.asarray(np.ascontiguousarray(xt.T))
 
@@ -196,12 +248,33 @@
     kp = jnp.kron(proj_weight.T, eye)
     kpt = jnp.kron(proj_weight, eye)
 
-    modes_shape = jax.ShapeDtypeStruct((xl, 2 * MZ, MY * C), f32)
     field_spec = plane((C, NY, NZ))
-    modes_spec = plane((2 * MZ, MY * C))
+    EX = -(-C // (2 * HZ)) if direct else 0
+    if direct:
+        modes_shape = jax.ShapeDtypeStruct((gx, xl, 2, HZ, 128), f32)
+        sums_shape = jax.ShapeDtypeStruct((gx, xl + EX, 2, HZ, 128), f32)
+        modes_spec = pl.BlockSpec((gx, 1, 2, HZ, 128), lambda i: (0, i, 0, 0, 0))
+    else:
+        modes_shape = jax.ShapeDtypeStruct((xl, 2 * MZ, MY * C), f32)
+        sums_shape = modes_shape
+        modes_spec = plane((2 * MZ, MY * C))
     vel_spec = plane((3, NY, NZ))
 
+    def exchange(slab):
+        return lax.all_to_all(slab, "gx", split_axis=0, concat_axis=0, tiled=True)
+
+    def x_modes(slab):
+        out = pl.pallas_call(
+            x_forward_body,
+            out_shape=jax.ShapeDtypeStruct((HZ, 2 * MX, 128), f32),
+            compiler_params=pltpu.CompilerParams(vmem_limit_bytes=32 * 1024 * 1024),
+        )(slab, x_forward)
+        out = out.reshape(HZ, MX, 2, PK, KY, C).transpose(1, 2, 4, 0, 3, 5)
+        return out.reshape(MX, 2, PL, C)
+
     def to_owner(slab):
+        if direct:
+            return x_modes(exchange(slab))
         slab = slab.reshape(xl, 2, MZ, MY, C).transpose(3, 2, 1, 0, 4)
         slab = slab.reshape(gx, PL, 2, xl, C).transpose(0, 2, 3, 1, 4)
         slab = slab.reshape(gx, 2 * xl, PL * C)
@@ -210,6 +283,14 @@
         return out.reshape(MX, 2, PL, C)
 
     def to_planes(modes):
+        if direct:
+            out = modes.reshape(MX, 2, KY, HZ, PK, C).transpose(3, 0, 1, 4, 2, 5)
+            out = pl.pallas_call(
+                x_back_body,
+                out_shape=modes_shape,
+                compiler_params=pltpu.CompilerParams(vmem_limit_bytes=32 * 1024 * 1024),
+            )(out.reshape(HZ, 2 * MX, 128), x_back)
+            return exchange(out)
         out = jnp.dot(x_back, modes.reshape(2 * MX, PL * C), precision=precise)
         out = out.reshape(gx, 2 * xl, PL * C)
         out = lax.all_to_all(out, "gx", split_axis=0, concat_axis=0, tiled=True)
@@ -230,16 +311,15 @@
         compiler_params=params,
     )(fields, ty, zt)
     spectrum = to_owner(slab)
-    weights = lax.all_gather(spectral_weight, "rep", axis=0, tiled=True).astype(f32)
-    w_re, w_im = weights[:, :, 0], weights[:, :, 1]
-    s_re, s_im = spectrum[:, 0], spectrum[:, 1]
-
-    def apply(w, s):
-        return jnp.einsum("mpoc,mpc->mpo", w, s, precision=precise)
-
+    weights = lax.all_gather(spectral_weight, "rep", axis=0, tiled=True)
+    weights = weights.transpose(2, 3, 4, 0, 1).reshape(2, C, C, MX * PL)
+    w_re, w_im = lax.optimization_barrier(weights).astype(f32)
+    turned = spectrum.transpose(1, 3, 0, 2).reshape(2, 1, C, MX * PL)
+    s_re, s_im = turned[0], turned[1]
     product = jnp.stack(
-        [apply(w_re, s_re) - apply(w_im, s_im), apply(w_re, s_im) + apply(w_im, s_re)], axis=1
-    )
+        [jnp.sum(w_re * s_re - w_im * s_im, axis=1), jnp.sum(w_re * s_im + w_im * s_re, axis=1)]
+    )
+    product = product.reshape(2, C, MX, PL).transpose(2, 0, 3, 1)
     wave = to_planes(product)
     spectra = both_samples(spectrum)
 
@@ -283,7 +363,7 @@
         backward_body,
         grid=(xl,),
         out_shape=(
-            modes_shape,
+            sums_shape,
             jax.ShapeDtypeStruct((wide, wide), f32),
             jax.ShapeDtypeStruct((wide, 3 * ROWS), f32),
         ),
@@ -300,30 +380,47 @@
         compiler_params=params,
     )(fields, pre, grad_vel, ty, zt, kpt)
 
-    grads = both_samples(to_owner(grad_slab))
-
     gather = jnp.asarray(np.kron(np.eye(C), np.ones((1, ROWS))).astype(np.float32))
     gather_q = jnp.asarray(np.kron(np.eye(3), np.ones((ROWS, 1))).astype(np.float32))
     mask = jnp.asarray(np.kron(np.ones((C, C)), np.eye(ROWS)).astype(np.float32))
     mask_q = jnp.asarray(np.kron(np.ones((C, 3)), np.eye(ROWS)).astype(np.float32))
     grad_w = jnp.dot(jnp.dot(gather, gw * mask, precision=precise), gather.T, precision=precise)
     grad_q = jnp.dot(jnp.dot(gather, gq * mask_q, precision=precise), gather_q, precision=precise)
-    packed = jnp.concatenate([grad_w.reshape(-1), grad_q.reshape(-1), loss_sum.reshape(1)])
-    packed = lax.psum(packed, ("gx", "rep"))
-    grad_w = packed[: C * C].reshape(C, C) * scale
-    grad_q = packed[C * C : C * C + 3 * C].reshape(C, 3) * scale
-    loss = packed[-1:] / (rep * NX * NY * NZ)
+    if direct:
+        last = jnp.broadcast_to(loss_sum.reshape(1, 1), (C, 1))
+        packed = jnp.concatenate([grad_w, grad_q, last], axis=1)
+        packed = jnp.pad(packed, ((0, 0), (0, 128 - C - 4)))
+        packed = jnp.pad(packed.reshape(-1), (0, EX * 2 * HZ * 128 - C * 128))
+        packed = jnp.broadcast_to(packed.reshape(1, EX, 2, HZ, 128), (gx, EX, 2, HZ, 128))
+        slab = exchange(lax.dynamic_update_slice(grad_slab, packed, (0, xl, 0, 0, 0)))
+        grads = x_modes(slab)
+        sums = jnp.sum(slab[:, xl:], axis=0).reshape(-1)
+        both = jnp.concatenate(
+            [grads.reshape(rep, -1), jnp.broadcast_to(sums[None], (rep, sums.size))], axis=1
+        )
+        both = lax.all_to_all(both, "rep", split_axis=0, concat_axis=0, tiled=True)
+        size = grads.size // rep
+        grads = both[:, :size].reshape(rep, MX // rep, 2, PL, C)
+        sums = jnp.sum(both[:, size:], axis=0)[: C * 128].reshape(C, 128)
+        grad_w, grad_q, loss = sums[:, :C], sums[:, C : C + 3], sums[0, C + 3 : C + 4]
+    else:
+        grads = both_samples(to_owner(grad_slab))
+        packed = jnp.concatenate([grad_w.reshape(-1), grad_q.reshape(-1), loss_sum.reshape(1)])
+        packed = lax.psum(packed, ("gx", "rep"))
+        grad_w = packed[: C * C].reshape(C, C)
+        grad_q = packed[C * C : C * C + 3 * C].reshape(C, 3)
+        loss = packed[-1:]
+    loss = loss / (rep * NX * NY * NZ)
 
     g_re, g_im = grads[:, :, 0], grads[:, :, 1]
-    s_re, s_im = spectra[:, :, 0], spectra[:, :, 1]
-
-    def outer(g, s):
-        return jnp.sum(g[..., :, None] * s[..., None, :], axis=0)
-
-    grad_r = jnp.stack(
-        [outer(g_re, s_re) + outer(g_im, s_im), outer(g_im, s_re) - outer(g_re, s_im)], axis=2
-    )
-    return (penalty[None], grad_r, grad_w, grad_q, loss)
+    across = jnp.stack([jnp.stack([g_re, g_im], 3), jnp.stack([g_im, -g_re], 3)], 1)
+    terms = [
+        across[b, t][..., None] * spectra[b, :, t][:, :, None, None, :]
+        for b in range(rep)
+        for t in range(2)
+    ]
+    grad_r = sum(terms[1:], terms[0])
+    return (penalty[None], grad_r, grad_w * scale, grad_q * scale, loss)
 
 
 def solution(mesh):

time: 413 us -> 323 us (0.78); the launches traced: 405 us -> 322 us
  local copies, waits for them, and re-layouts: 85.6 us -> 24.9 us
  matrix products: 36.2 us -> 3.53 us
  other arithmetic: 29.6 us -> 44.9 us
  Pallas kernels: 125 us -> 133 us
  starting transfers between devices: 23.2 us -> 15.2 us
    reshape x12 -> x6, local copies, waits for them, and re-layouts: 42 us -> 1.92 us  [the longest x4 1.25 us: x_modes(): out = out.reshape(HZ, MX, 2, PK, KY, C).transpose(1, 2, 4, 0, 3, 5)]
    psum x1 -> x0, blocking collectives: 36.2 us -> none  [local(): packed = lax.psum(packed, ('gx', 'rep'))]
    dot_general x7 -> x0, matrix products: 33.3 us -> none  [the longest x4 30 us: apply(): return jnp.einsum('mpoc,mpc->mpo', w, s, precision=precise)]
    all_to_all x1 -> x2, blocking collectives: 3.84 us -> 36.8 us  [the longest x1 33 us: exchange(): return lax.all_to_all(slab, 'gx', split_axis=0, concat_axis=0, tiled=True)]
    transpose x4 -> x2, local copies, waits for them, and re-layouts: 17.8 us -> 0.76 us  [the longest x1 0.41 us: to_planes(): out = modes.reshape(MX, 2, KY, HZ, PK, C).transpose(3, 0, 1, 4, 2, 5)]
    convert_element_type x0 -> x1, other arithmetic: none -> 11.5 us  [local(): w_re, w_im = lax.optimization_barrier(weights).astype(f32)]
    add x1, other arithmetic: 1.02 us -> 11 us  [local(): grad_r = sum(terms[1:], terms[0])]
    all_to_all x3 -> x2, starting transfers between devices: 14.9 us -> 7.37 us  [exchange(): return lax.all_to_all(slab, 'gx', split_axis=0, concat_axis=0, tiled=True)]
  transfers between devices with their start and end apart: 9 -> 8, of which waited for: 6 -> 5; matrix products, arithmetic and copies ran while one was open for 18% -> 11% of each run, Pallas kernels for 27% -> 40%
where the time goes in v2:
time: 323 us; the launch traced here: 322 us
  Pallas kernels  133 us (41%)
  waiting for transfers between devices  45 us (14%)
  other arithmetic  44.9 us (14%)
  blocking collectives  36.8 us (11%)
  local copies, waits for them, and re-layouts  24.9 us (8%)
  between operations  18.5 us (6%)
  starting transfers between devices  15.2 us (5%)
  matrix products  3.53 us (1%)
    pallas_call x1, Pallas kernels, local(): pl.pallas_call(backward_body, grid=(xl,), out_shape=(sums_shape, jax.Shap...  59.3 us
    pallas_call x1, Pallas kernels, local(): pl.pallas_call(functools.partial(middle_body, scale), grid=(xl,), out_sha...  51.4 us
    all_to_all x2, waiting for transfers between devices, exchange(): return lax.all_to_all(slab, 'gx', split_axis=0, concat_axis=0, tiled=True)  35.8 us
    all_to_all x1, blocking collectives, exchange(): return lax.all_to_all(slab, 'gx', split_axis=0, concat_axis=0, tiled=True)  33 us
    pallas_call x1, Pallas kernels, local(): pl.pallas_call(forward_body, grid=(xl,), out_shape=modes_shape, in_specs=...  18.8 us
    convert_element_type x1, other arithmetic, local(): w_re, w_im = lax.optimization_barrier(weights).astype(f32)  11.5 us
    add x1, other arithmetic, local(): grad_r = sum(terms[1:], terms[0])  11 us
    mul x1, local copies, waits for them, and re-layouts, local(): kw = jnp.kron(local_weight.T, eye)  8.42 us
  transfers between devices with their start and end apart: 8, of which 5 were waited for; matrix products, arithmetic and copies ran while one was open for 11% of the time, Pallas kernels for 40%

profile of v2, /device:TPU:0, one launch (start us, length us, event | category | flops | bytes accessed | tf_op | source)
XLA Modules:
  0.0 321.6 jit_solution(1629364621780742158)
XLA Ops:
  7.9 18.8 %shard_map.191 = f32[8,16,2,8,128]{4,3,2,1,0:T(8,128)} custom-call(bf16[16,32,128,128]{3,2,1,0:T(8,128)(2,1)} %bitcast.144, bf16[32,128]{1,0:T(8,128)(2,1)} %constant.45.clone.ty_ref, bf16[64,256]{1,0:T(8,128)(2,1)} %constant.47.clone.zt_ref), custom_call_target="tpu_custom_call" | custom-call | tf_op jit(solution)/shard_map/pallas_call | solution.py:305
  26.7 33.0 %all_to_all.32.slab_ref = f32[8,16,2,8,128]{4,3,2,1,0:T(8,128)S(1)} all-to-all(f32[8,16,2,8,128]{4,3,2,1,0:T(8,128)} %shard_map.191), channel_id=1, replica_groups=mesh['grp'=2,'gx'=8,'rep'=2] {'gx'}, dimensions={0} | all-to-all | bytes 2097152 | tf_op jit(solution)/shard_map/all_to_all | solution.py:264
  61.1 11.5 %copy_convert_fusion = f32[2,32,32,512]{2,1,3,0:T(8,128)} fusion(bf16[2,32,32,512]{2,1,0,3:T(8,128)(2,1)} %bitcast.148), kind=kLoop, calls=%fused_computation.2 | loop fusion | flops 1048576 | bytes 6291456 | tf_op jit(solution)/shard_map/convert_element_type | solution.py:316
  72.7 8.1 %subtract_reduce_fusion = (f32[32,512]{0,1:T(8,128)S(1)}, f32[32,512]{0,1:T(8,128)S(1)}) fusion(f32[2,32,32,512]{2,1,3,0:T(8,128)} %copy_convert_fusion, f32[32,512]{0,1:T(8,128)S(1)} %bitcast.155, f32[32,512]{0,1:T(8,128)S(1)} %bitcast.156), kind=kLoop, calls=%fused_computation.5 | loop fusion | flops 4161536 | bytes 4456448 | tf_op jit(solution)/shard_map/reduce_sum | solution.py:320
  82.4 2.0 shard_map.193
  84.4 3.6 %all-to-all-start.1 = ((f32[8,16,2,8,128]{4,3,2,1,0:T(8,128)}), f32[8,16,2,8,128]{4,3,2,1,0:T(8,128)S(1)}, u32[]{:S(2)}, u32[]{:S(2)}) async-start(f32[8,16,2,8,128]{4,3,2,1,0:T(8,128)} %shard_map.193), calls=%async_computation.1 | async-start | bytes 2097152 | tf_op jit(solution)/shard_map/all_to_all | solution.py:264
  88.2 2.4 broadcast_multiply_fusion
  90.6 8.4 %mul.246.kw_ref = bf16[512,512]{1,0:T(8,128)(2,1)} reshape(bf16[32,16,32,16]{3,2,1,0:T(8,128)(2,1)} %broadcast_multiply_fusion) | data formatting | bytes 1048576 | tf_op jit(solution)/shard_map/jit(kron)/mul | solution.py:247
  99.1 1.1 mul.250.kp_ref
  101.6 0.9 reshape.246
  102.5 11.2 %all-to-all-done.1.m_ref = f32[8,16,2,8,128]{4,3,2,1,0:T(8,128)S(1)} async-done(((f32[8,16,2,8,128]{4,3,2,1,0:T(8,128)}), f32[8,16,2,8,128]{4,3,2,1,0:T(8,128)S(1)}, u32[]{:S(2)}, u32[]{:S(2)}) %all-to-all-start.1) | async-done | bytes 1048608 | tf_op jit(solution)/shard_map/all_to_all | solution.py:264
  113.6 3.6 %all-to-all-start.4 = ((f32[2,1,16384]{2,1,0:T(1,128)}), f32[2,1,16384]{2,1,0:T(1,128)S(1)}, u32[]{:S(2)}, u32[]{:S(2)}) async-start(f32[2,1,16384]{2,1,0:T(1,128)} %reshape.246), calls=%async_computation.4 | async-start | bytes 262144 | tf_op jit(solution)/shard_map/all_to_all | solution.py:303
  117.2 51.4 %shard_map.194 = (f32[16,32,128,128]{3,2,1,0:T(8,128)}, f32[16,3,128,128]{3,2,1,0:T(8,128)}) custom-call(bf16[16,32,128,128]{3,2,1,0:T(8,128)(2,1)} %bitcast.145, f32[8,16,2,8,128]{4,3,2,1,0:T(8,128)} %copy-done.5, bf16[96,256]{1,0:T(8,128)(2,1)} %constant.48.clone.zi_ref, bf16[128,32]{1,0:T(8,128)(2,1)} %constant.46.clone.yi_ref, ...), custom_call_target="tpu_custom_call" | custom-call | tf_op jit(solution)/shard_map/pallas_call | solution.py:326
  168.6 1.7 slice_bitcast_fusion.9
  171.0 1.2 copy-done.3
  172.7 2.2 collective-permute-start.1
  174.9 1.8 collective-permute-done.1
  176.7 4.8 %collective-permute-done = bf16[1,128,128]{2,1,0:T(8,128)(2,1)S(1)} collective-permute-done((bf16[1,128,128]{2,1,0:T(8,128)(2,1)S(1)}, bf16[1,128,128]{2,1,0:T(8,128)(2,1)S(1)}, u32[]{:S(2)}, u32[]{:S(2)}) %collective-permute-start) | collective-permute-done | bytes 32800 | tf_op jit(solution)/shard_map/ppermute | solution.py:203
  181.6 1.5 multiply_reduce_fusion.1
  184.8 2.0 collective-permute-start.2
  186.8 2.0 fusion.7
  189.6 1.8 collective-permute-done.2
  191.5 1.1 maximum_convert_fusion.1
  192.7 4.3 %multiply_reduce_fusion = (f32[]{:T(128)}, bf16[16,3,128,128]{3,2,1,0:T(8,128)(2,1)}) fusion(f32[16,3,128,128]{3,2,1,0:T(8,128)S(1)} %copy-done.4, bf16[1,16,3,128,128]{4,3,2,1,0:T(8,128)(2,1)} %param.17, f32[16,1,128,128]{3,2,1,0:T(8,128)} %get-tuple-element.81, f32[16,1,128,128]{3,2,1,0:T(8,128)S(1)} %copy-done.7, f32[16,1,128,128]{3,2,1,0:T(8,128)S(1)} %fusion.3), kind=kLoop, calls=%fused_computation.10 | loop fusion | flops 7864319 | bytes 9437188 | tf_op jit(solution)/shard_map/reduce_sum | solution.py:352
  197.0 59.3 %shard_map.195 = (f32[8,18,2,8,128]{4,3,2,1,0:T(8,128)}, f32[512,512]{1,0:T(8,128)}, f32[512,48]{1,0:T(8,128)}) custom-call(bf16[16,32,128,128]{3,2,1,0:T(8,128)(2,1)} %bitcast.146, f32[16,32,128,128]{3,2,1,0:T(8,128)} %get-tuple-element.11.pre_ref, bf16[16,3,128,128]{3,2,1,0:T(8,128)(2,1)} %get-tuple-element.43.gv_ref, ...), custom_call_target="tpu_custom_call" | custom-call | tf_op jit(solution)/shard_map/pallas_call | solution.py:362
  256.3 2.0 fusion.11
  258.5 1.2 fusion.19
  262.1 3.8 %all-to-all-start.2 = ((f32[8,18,2,8,128]{4,3,2,1,0:T(8,128)}), f32[8,18,2,8,128]{4,3,2,1,0:T(8,128)S(1)}, u32[]{:S(2)}, u32[]{:S(2)}) async-start(f32[8,18,2,8,128]{4,3,2,1,0:T(8,128)} %broadcast_dynamic-update-slice_fusion), calls=%async_computation.2 | async-start | bytes 2359296 | tf_op jit(solution)/shard_map/all_to_all | solution.py:264
  266.4 1.0 reduce
  267.8 24.7 %all-to-all-done.2.slab_ref = f32[8,18,2,8,128]{4,3,2,1,0:T(8,128)S(1)} async-done(((f32[8,18,2,8,128]{4,3,2,1,0:T(8,128)}), f32[8,18,2,8,128]{4,3,2,1,0:T(8,128)S(1)}, u32[]{:S(2)}, u32[]{:S(2)}) %all-to-all-start.2) | async-done | bytes 1179680 | tf_op jit(solution)/shard_map/all_to_all | solution.py:264
  294.7 3.8 %all_to_all.33 = f32[2,1,20480]{2,1,0:T(1,128)S(1)} all-to-all(f32[2,1,20480]{2,1,0:T(1,128)S(1)} %copy.121), channel_id=1, replica_groups=mesh['grp'=2,'gx'=8,'rep'=2] {'rep'}, dimensions={0} | all-to-all | bytes 327680 | tf_op jit(solution)/shard_map/all_to_all | solution.py:401
  302.6 11.0 %multiply_add_fusion = f32[8,32,2,32,32]{4,3,2,1,0:T(8,128)} fusion(f32[8,32,32]{2,1,0:T(8,128)S(1)} %copy.131, f32[8,32,2,32]{3,2,1,0:T(2,128)S(1)} %copy.130, f32[8,32,32]{2,1,0:T(8,128)S(1)} %copy.129, f32[8,32,2,32]{3,2,1,0:T(2,128)S(1)} %copy.128, f32[8,32,32]{2,1,0:T(8,128)S(1)} %copy.127, f32[8,32,2,32]{3,2,1,0:T(2,128)S(1)} %copy.126, ...), kind=kLoop, calls=%fused_computation.3 | loop fusion | flops 3670016 | bytes 2490368 | tf_op jit(solution)/shard_map/add | solution.py:422
  (107 shorter events, 16.0 us)
Async XLA Ops:
  7.2 54.0 %all-gather.2.cloned.1.call-start = ((), (), s32[]{:S(2)}) async-start(), calls=%async_computation.5 | async-start | bytes 12582912 | tf_op jit(solution)/shard_map/all_gather | solution.py:314
  7.9 51.7 %copy-start.1 = (f32[32,256]{1,0:T(8,128)S(1)}, f32[32,256]{1,0:T(8,128)}, u32[]{:S(2)}) copy-start(f32[32,256]{1,0:T(8,128)} %constant.49.clone.table_ref) | copy-start | bytes 98308
  80.8 1.6 copy-start
  80.8 7.3 %copy-start.13 = (bf16[32,32]{1,0:T(8,128)(2,1)S(1)}, bf16[32,32]{1,0:T(8,128)(2,1)}, u32[]{:S(2)}) copy-start(bf16[32,32]{1,0:T(8,128)(2,1)} %param.19) | copy-start | bytes 6148
  84.4 29.2 %all-to-all-start.1 = ((f32[8,16,2,8,128]{4,3,2,1,0:T(8,128)}), f32[8,16,2,8,128]{4,3,2,1,0:T(8,128)S(1)}, u32[]{:S(2)}, u32[]{:S(2)}) async-start(f32[8,16,2,8,128]{4,3,2,1,0:T(8,128)} %shard_map.193), calls=%async_computation.1 | async-start | bytes 2097152 | tf_op jit(solution)/shard_map/all_to_all | solution.py:264
  88.2 10.8 %copy-start.14 = (bf16[32,3]{0,1:T(4,128)(2,1)S(1)}, bf16[32,3]{0,1:T(4,128)(2,1)}, u32[]{:S(2)}) copy-start(bf16[32,3]{0,1:T(4,128)(2,1)} %param.20) | copy-start | bytes 580
  113.6 3.6 %copy-start.5 = (f32[8,16,2,8,128]{4,3,2,1,0:T(8,128)}, f32[8,16,2,8,128]{4,3,2,1,0:T(8,128)S(1)}, u32[]{:S(2)}) copy-start(f32[8,16,2,8,128]{4,3,2,1,0:T(8,128)S(1)} %all-to-all-done.1.m_ref) | copy-start | bytes 3145732
  113.6 148.4 %all-to-all-start.4 = ((f32[2,1,16384]{2,1,0:T(1,128)}), f32[2,1,16384]{2,1,0:T(1,128)S(1)}, u32[]{:S(2)}, u32[]{:S(2)}) async-start(f32[2,1,16384]{2,1,0:T(1,128)} %reshape.246), calls=%async_computation.4 | async-start | bytes 262144 | tf_op jit(solution)/shard_map/all_to_all | solution.py:303
  170.3 1.9 copy-start.3
  172.5 9.2 %copy-start.6 = (s32[1,16,128,128]{3,2,1,0:T(8,128)S(1)}, s32[1,16,128,128]{3,2,1,0:T(8,128)}, u32[]{:S(2)}) copy-start(s32[1,16,128,128]{3,2,1,0:T(8,128)} %param.18) | copy-start | bytes 3145732
  172.7 4.0 %collective-permute-start.1 = (bf16[1,128,128]{2,1,0:T(8,128)(2,1)S(1)}, bf16[1,128,128]{2,1,0:T(8,128)(2,1)S(1)}, u32[]{:S(2)}, u32[]{:S(2)}) collective-permute-start(bf16[1,128,128]{2,1,0:T(8,128)(2,1)S(1)} %get-tuple-element.47), channel_id=1, source_target_pairs={{2,0},{4,2},{6,4},{8,6},{10,8},{12,10},{14,12},{0,14},{3,1},{5,3},... | collective-permute-start | bytes 98312 | tf_op jit(solution)/shard_map/ppermute | solution.py:204
  174.9 6.6 %collective-permute-start = (bf16[1,128,128]{2,1,0:T(8,128)(2,1)S(1)}, bf16[1,128,128]{2,1,0:T(8,128)(2,1)S(1)}, u32[]{:S(2)}, u32[]{:S(2)}) collective-permute-start(bf16[1,128,128]{2,1,0:T(8,128)(2,1)S(1)} %get-tuple-element.46), channel_id=1, source_target_pairs={{0,2},{2,4},{4,6},{6,8},{8,10},{10,12},{12,14},{14,0},{1,3},{3,5},... | collective-permute-start | bytes 98312 | tf_op jit(solution)/shard_map/ppermute | solution.py:203
  183.4 1.0 copy-start.2
  183.4 1.3 copy-start.8
  184.7 4.9 %collective-permute-start.3 = (bf16[1,128,128]{2,1,0:T(8,128)(2,1)S(1)}, bf16[1,128,128]{2,1,0:T(8,128)(2,1)S(1)}, u32[]{:S(2)}, u32[]{:S(2)}) collective-permute-start(bf16[1,128,128]{2,1,0:T(8,128)(2,1)S(1)} %get-tuple-element.75), channel_id=1, source_target_pairs={{2,0},{4,2},{6,4},{8,6},{10,8},{12,10},{14,12},{0,14},{3,1},{5,3},... | collective-permute-start | bytes 98312 | tf_op jit(solution)/shard_map/ppermute | solution.py:204
  184.8 6.7 %collective-permute-start.2 = (bf16[1,128,128]{2,1,0:T(8,128)(2,1)S(1)}, bf16[1,128,128]{2,1,0:T(8,128)(2,1)S(1)}, u32[]{:S(2)}, u32[]{:S(2)}) collective-permute-start(bf16[1,128,128]{2,1,0:T(8,128)(2,1)S(1)} %get-tuple-element.74), channel_id=1, source_target_pairs={{0,2},{2,4},{4,6},{6,8},{8,10},{10,12},{12,14},{14,0},{1,3},{3,5},... | collective-permute-start | bytes 98312 | tf_op jit(solution)/shard_map/ppermute | solution.py:203
  188.8 3.9 %copy-start.4 = (f32[16,3,128,128]{3,2,1,0:T(8,128)S(1)}, f32[16,3,128,128]{3,2,1,0:T(8,128)}, u32[]{:S(2)}) copy-start(f32[16,3,128,128]{3,2,1,0:T(8,128)} %get-tuple-element.10) | copy-start | bytes 9437188
  189.6 3.1 copy-start.7
  197.0 59.3 %copy-start.9 = (f32[512,512]{1,0:T(8,128)S(1)}, f32[512,512]{1,0:T(8,128)}, u32[]{:S(2)}) copy-start(f32[512,512]{1,0:T(8,128)} %constant.53.clone) | copy-start | bytes 3145732
  197.0 59.3 %copy-start.10 = (f32[32,512]{1,0:T(8,128)S(1)}, f32[32,512]{1,0:T(8,128)}, u32[]{:S(2)}) copy-start(f32[32,512]{1,0:T(8,128)} %constant.51.clone) | copy-start | bytes 196612
  197.0 61.5 %copy-start.11 = (f32[512,48]{1,0:T(8,128)S(1)}, f32[512,48]{1,0:T(8,128)}, u32[]{:S(2)}) copy-start(f32[512,48]{1,0:T(8,128)} %constant.54.clone) | copy-start | bytes 294916
  197.0 62.7 %copy-start.12 = (f32[48,3]{1,0:T(8,128)S(1)}, f32[48,3]{1,0:T(8,128)}, u32[]{:S(2)}) copy-start(f32[48,3]{1,0:T(8,128)} %constant.52.clone) | copy-start | bytes 1732
  262.1 30.4 %all-to-all-start.2 = ((f32[8,18,2,8,128]{4,3,2,1,0:T(8,128)}), f32[8,18,2,8,128]{4,3,2,1,0:T(8,128)S(1)}, u32[]{:S(2)}, u32[]{:S(2)}) async-start(f32[8,18,2,8,128]{4,3,2,1,0:T(8,128)} %broadcast_dynamic-update-slice_fusion), calls=%async_computation.2 | async-start | bytes 2359296 | tf_op jit(solution)/shard_map/all_to_all | solution.py:264
Sparse Core Ops, SparseCore 0:
  9.5 22.5 all-gather.1

commit v3 on v2

--- a/solution.py
+++ b/solution.py
@@ -54,9 +54,12 @@
 
 
 def plane_modes(load, count, ty, zt):
-    parts = jnp.stack([dot(ty, load(c)) for c in range(count)], axis=0)
-    turned = jnp.swapaxes(parts, 0, 1)
-    nz = turned.shape[-1]
+    parts = []
+    for c in range(0, count, 2):
+        pair = dot(ty, jnp.concatenate([load(c), load(c + 1)], axis=1))
+        nz = pair.shape[1] // 2
+        parts += [pair[:, :nz], pair[:, nz:]]
+    turned = jnp.swapaxes(jnp.stack(parts, axis=0), 0, 1)
     real = turned[:MY].reshape(MY * count, nz)
     imag = turned[MY:].reshape(MY * count, nz)
     high, low = split(jnp.concatenate([real, imag], axis=1))
@@ -145,13 +148,12 @@
         pre_ref[0, o] = both[:, :nz] * scale
         pre_ref[0, o + 1] = both[:, nz:] * scale
 
-    @pl.loop(0, ny // (2 * ROWS))
-    def _(step):
-        y0 = pl.multiple_of(step * 2 * ROWS, 2 * ROWS)
+    for y0 in range(0, ny, 2 * ROWS):
         x = tile_pair(pre_ref, y0) + dot(kw_ref[...], tile_pair(f_ref, y0))
         put_pair(pre_ref, y0, x)
-        t = jnp.tanh(ROOT * (x + 0.044715 * (x * x * x)))
-        hidden = (x * (0.5 * (1.0 + t))).astype(bf16)
+        t = jnp.tanh(x * (ROOT + (0.044715 * ROOT) * (x * x)))
+        half = 0.5 * x
+        hidden = (half + half * t).astype(bf16)
         put_pair(vel_ref, y0, dot(kp_ref[...], hidden))
 
 
@@ -165,20 +167,23 @@
         gw_ref[...] = jnp.zeros_like(gw_ref)
         gq_ref[...] = jnp.zeros_like(gq_ref)
 
-    @pl.loop(0, ny // (2 * ROWS))
-    def _(step):
-        y0 = pl.multiple_of(step * 2 * ROWS, 2 * ROWS)
+    hiddens, grads, fields, slopes = [], [], [], []
+    for y0 in range(0, ny, 2 * ROWS):
         gv = tile_pair(gv_ref, y0)
         x = tile_pair(pre_ref, y0)
-        xx = x * x
-        t = jnp.tanh(ROOT * (x + 0.044715 * (xx * x)))
-        cdf = 0.5 * (1.0 + t)
+        cubic = (0.044715 * ROOT) * (x * x)
+        t = jnp.tanh(x * (ROOT + cubic))
+        cdf = 0.5 + 0.5 * t
         hidden = (x * cdf).astype(bf16)
-        slope = cdf + x * (0.5 * (1.0 - t * t)) * (ROOT + (3.0 * 0.044715 * ROOT) * xx)
+        slope = cdf + (x * (ROOT + 3.0 * cubic)) * (0.5 - 0.5 * (t * t))
         gp = (dot(kpt_ref[...], gv) * slope).astype(bf16)
         put_pair(gp_ref, y0, gp)
-        gw_ref[...] += dot_nt(tile_pair(f_ref, y0), gp)
-        gq_ref[...] += dot_nt(hidden, gv)
+        hiddens.append(hidden)
+        grads.append(gp)
+        slopes.append(gv)
+        fields.append(tile_pair(f_ref, y0))
+    gw_ref[...] += dot_nt(jnp.concatenate(fields, axis=1), jnp.concatenate(grads, axis=1))
+    gq_ref[...] += dot_nt(jnp.concatenate(hiddens, axis=1), jnp.concatenate(slopes, axis=1))
 
     store_modes(out_ref, plane_modes(lambda c: gp_ref[0, c], count, ty_ref[...], zt_ref[...]))
 
@@ -310,16 +315,21 @@
         out_specs=modes_spec,
         compiler_params=params,
     )(fields, ty, zt)
+    slab, weights = lax.optimization_barrier((slab, spectral_weight))
+    weights = weights.transpose(2, 3, 4, 0, 1).reshape(1, 2, C, C, MX // rep * PL)
+    weights = lax.all_gather(weights, "rep", axis=0, tiled=True)
     spectrum = to_owner(slab)
-    weights = lax.all_gather(spectral_weight, "rep", axis=0, tiled=True)
-    weights = weights.transpose(2, 3, 4, 0, 1).reshape(2, C, C, MX * PL)
-    w_re, w_im = lax.optimization_barrier(weights).astype(f32)
-    turned = spectrum.transpose(1, 3, 0, 2).reshape(2, 1, C, MX * PL)
-    s_re, s_im = turned[0], turned[1]
+    KX = MX // rep
+    turned = spectrum.reshape(rep, KX, 2, PL, C).transpose(0, 2, 4, 1, 3)
+    turned = turned.reshape(rep, 2, 1, C, KX * PL)
+    w_re, w_im = weights[:, 0].astype(f32), weights[:, 1].astype(f32)
+    s_re, s_im = turned[:, 0], turned[:, 1]
     product = jnp.stack(
-        [jnp.sum(w_re * s_re - w_im * s_im, axis=1), jnp.sum(w_re * s_im + w_im * s_re, axis=1)]
-    )
-    product = product.reshape(2, C, MX, PL).transpose(2, 0, 3, 1)
+        [jnp.sum(w_re * s_re - w_im * s_im, axis=2), jnp.sum(w_re * s_im + w_im * s_re, axis=2)],
+        axis=1,
+    )
+    product = product.reshape(rep, 2, C, KX, PL).transpose(0, 3, 1, 4, 2)
+    product = product.reshape(MX, 2, PL, C)
     wave = to_planes(product)
     spectra = both_samples(spectrum)
 

time: 323 us -> 288 us (0.89)
  Pallas kernels: 133 us -> 111 us
  other arithmetic: 44.9 us -> 26.2 us
  local copies, waits for them, and re-layouts: 24.9 us -> 31.4 us
    pallas_call x1, Pallas kernels: 59.3 us -> 44.4 us  [local(): pl.pallas_call(backward_body, grid=(xl,), out_shape=(sums_shape, jax.Shap...]
    convert_element_type x1 -> x0, other arithmetic: 11.5 us -> none  [local(): w_re, w_im = lax.optimization_barrier(weights).astype(f32)]
    reshape x0 -> x2, local copies, waits for them, and re-layouts: none -> 5.92 us  [the longest x1 5.74 us: local(): weights.transpose(2, 3, 4, 0, 1).reshape(1, 2, C, C, MX // rep * PL)]
    reduce_sum x1, other arithmetic: 8.13 us -> 2.57 us  [local(): jnp.sum(w_re * s_re - w_im * s_im, axis=2)]
    pallas_call x1, Pallas kernels: 51.4 us -> 46.2 us  [local(): pl.pallas_call(functools.partial(middle_body, scale), grid=(xl,), out_sha...]
  transfers between devices with their start and end apart: 8 -> 8, of which waited for: 5 -> 5; matrix products, arithmetic and copies ran while one was open for 11% -> 12% of each run, Pallas kernels for 40% -> 32%
where the time goes in v3:
time: 288 us; the launch traced here: 287 us
  Pallas kernels  111 us (39%)
  waiting for transfers between devices  44.3 us (15%)
  blocking collectives  36.7 us (13%)
  local copies, waits for them, and re-layouts  31.4 us (11%)
  other arithmetic  26.2 us (9%)
  between operations  18.4 us (6%)
  starting transfers between devices  15.2 us (5%)
  matrix products  3.53 us (1%)
    pallas_call x1, Pallas kernels, local(): pl.pallas_call(functools.partial(middle_body, scale), grid=(xl,), out_sha...  46.2 us
    pallas_call x1, Pallas kernels, local(): pl.pallas_call(backward_body, grid=(xl,), out_shape=(sums_shape, jax.Shap...  44.4 us
    all_to_all x2, waiting for transfers between devices, exchange(): return lax.all_to_all(slab, 'gx', split_axis=0, concat_axis=0, tiled=True)  35.7 us
    all_to_all x1, blocking collectives, exchange(): return lax.all_to_all(slab, 'gx', split_axis=0, concat_axis=0, tiled=True)  32.8 us
    pallas_call x1, Pallas kernels, local(): pl.pallas_call(forward_body, grid=(xl,), out_shape=modes_shape, in_specs=...  16.9 us
    add x1, other arithmetic, local(): grad_r = sum(terms[1:], terms[0])  11 us
    mul x1, local copies, waits for them, and re-layouts, local(): kw = jnp.kron(local_weight.T, eye)  8.42 us
    all_to_all x2, starting transfers between devices, exchange(): return lax.all_to_all(slab, 'gx', split_axis=0, concat_axis=0, tiled=True)  7.37 us
  transfers between devices with their start and end apart: 8, of which 5 were waited for; matrix products, arithmetic and copies ran while one was open for 12% of the time, Pallas kernels for 32%

profile of v3, /device:TPU:0, one launch (start us, length us, event | category | flops | bytes accessed | tf_op | source)
XLA Modules:
  0.0 286.6 jit_solution(2430654098666949523)
XLA Ops:
  7.2 16.9 %shard_map.191 = f32[8,16,2,8,128]{4,3,2,1,0:T(8,128)} custom-call(bf16[16,32,128,128]{3,2,1,0:T(8,128)(2,1)} %bitcast.150, bf16[32,128]{1,0:T(8,128)(2,1)} %constant.45.clone.ty_ref, bf16[64,256]{1,0:T(8,128)(2,1)} %constant.47.clone.zt_ref), custom_call_target="tpu_custom_call" | custom-call | tf_op jit(solution)/shard_map/pallas_call | solution.py:310
  24.1 5.7 %copy.133 = bf16[1,2,32,32,256]{4,3,2,1,0:T(8,128)(2,1)} copy(bf16[1,2,32,32,256]{3,2,1,4,0:T(8,128)(2,1)} %bitcast.156) | data formatting | bytes 2097152 | tf_op jit(solution)/shard_map/reshape | solution.py:319
  29.9 32.8 %all_to_all.32.slab_ref = f32[8,16,2,8,128]{4,3,2,1,0:T(8,128)S(1)} all-to-all(f32[8,16,2,8,128]{4,3,2,1,0:T(8,128)S(1)} %copy-done.5), channel_id=1, replica_groups=mesh['grp'=2,'gx'=8,'rep'=2] {'gx'}, dimensions={0} | all-to-all | bytes 2097152 | tf_op jit(solution)/shard_map/all_to_all | solution.py:269
  64.5 2.6 fusion.3
  68.9 2.0 shard_map.193
  70.9 3.6 %all-to-all-start.1 = ((f32[8,16,2,8,128]{4,3,2,1,0:T(8,128)}), f32[8,16,2,8,128]{4,3,2,1,0:T(8,128)S(1)}, u32[]{:S(2)}, u32[]{:S(2)}) async-start(f32[8,16,2,8,128]{4,3,2,1,0:T(8,128)} %shard_map.193), calls=%async_computation.1 | async-start | bytes 2097152 | tf_op jit(solution)/shard_map/all_to_all | solution.py:269
  74.7 2.4 broadcast_multiply_fusion
  77.0 8.4 %mul.246.kw_ref = bf16[512,512]{1,0:T(8,128)(2,1)} reshape(bf16[32,16,32,16]{3,2,1,0:T(8,128)(2,1)} %broadcast_multiply_fusion) | data formatting | bytes 1048576 | tf_op jit(solution)/shard_map/jit(kron)/mul | solution.py:252
  85.6 1.1 mul.250.kp_ref
  88.0 0.9 reshape.243
  88.9 11.2 %all-to-all-done.1.m_ref = f32[8,16,2,8,128]{4,3,2,1,0:T(8,128)S(1)} async-done(((f32[8,16,2,8,128]{4,3,2,1,0:T(8,128)}), f32[8,16,2,8,128]{4,3,2,1,0:T(8,128)S(1)}, u32[]{:S(2)}, u32[]{:S(2)}) %all-to-all-start.1) | async-done | bytes 1048608 | tf_op jit(solution)/shard_map/all_to_all | solution.py:269
  100.1 3.6 %all-to-all-start.4 = ((f32[2,1,16384]{2,1,0:T(1,128)}), f32[2,1,16384]{2,1,0:T(1,128)S(1)}, u32[]{:S(2)}, u32[]{:S(2)}) async-start(f32[2,1,16384]{2,1,0:T(1,128)} %reshape.243), calls=%async_computation.4 | async-start | bytes 262144 | tf_op jit(solution)/shard_map/all_to_all | solution.py:308
  103.7 46.2 %shard_map.194 = (f32[16,32,128,128]{3,2,1,0:T(8,128)}, f32[16,3,128,128]{3,2,1,0:T(8,128)}) custom-call(bf16[16,32,128,128]{3,2,1,0:T(8,128)(2,1)} %bitcast.151, f32[8,16,2,8,128]{4,3,2,1,0:T(8,128)} %copy-done.4, bf16[96,256]{1,0:T(8,128)(2,1)} %constant.48.clone.zi_ref, bf16[128,32]{1,0:T(8,128)(2,1)} %constant.46.clone.yi_ref, ...), custom_call_target="tpu_custom_call" | custom-call | tf_op jit(solution)/shard_map/pallas_call | solution.py:336
  149.9 1.7 slice_bitcast_fusion.7
  152.3 1.5 copy-done.3
  154.4 2.2 collective-permute-start.1
  156.6 1.8 collective-permute-done.1
  158.3 4.8 %collective-permute-done = bf16[1,128,128]{2,1,0:T(8,128)(2,1)S(1)} collective-permute-done((bf16[1,128,128]{2,1,0:T(8,128)(2,1)S(1)}, bf16[1,128,128]{2,1,0:T(8,128)(2,1)S(1)}, u32[]{:S(2)}, u32[]{:S(2)}) %collective-permute-start) | collective-permute-done | bytes 32800 | tf_op jit(solution)/shard_map/ppermute | solution.py:208
  163.3 1.5 multiply_reduce_fusion.1
  166.4 2.0 collective-permute-start.2
  168.4 2.0 fusion.11
  171.1 2.0 collective-permute-done.2
  173.1 1.1 maximum_convert_fusion.1
  174.3 2.7 multiply_reduce_fusion
  177.0 44.4 %shard_map.195 = (f32[8,18,2,8,128]{4,3,2,1,0:T(8,128)}, f32[512,512]{1,0:T(8,128)}, f32[512,48]{1,0:T(8,128)}) custom-call(bf16[16,32,128,128]{3,2,1,0:T(8,128)(2,1)} %bitcast.152, f32[16,32,128,128]{3,2,1,0:T(8,128)} %get-tuple-element.15.pre_ref, bf16[16,3,128,128]{3,2,1,0:T(8,128)(2,1)} %get-tuple-element.47.gv_ref, ...), custom_call_target="tpu_custom_call" | custom-call | tf_op jit(solution)/shard_map/pallas_call | solution.py:372
  221.4 2.0 fusion.15
  223.6 1.2 fusion.23
  227.2 3.8 %all-to-all-start.2 = ((f32[8,18,2,8,128]{4,3,2,1,0:T(8,128)}), f32[8,18,2,8,128]{4,3,2,1,0:T(8,128)S(1)}, u32[]{:S(2)}, u32[]{:S(2)}) async-start(f32[8,18,2,8,128]{4,3,2,1,0:T(8,128)} %broadcast_dynamic-update-slice_fusion), calls=%async_computation.2 | async-start | bytes 2359296 | tf_op jit(solution)/shard_map/all_to_all | solution.py:269
  231.5 1.0 reduce
  232.9 24.6 %all-to-all-done.2.slab_ref = f32[8,18,2,8,128]{4,3,2,1,0:T(8,128)S(1)} async-done(((f32[8,18,2,8,128]{4,3,2,1,0:T(8,128)}), f32[8,18,2,8,128]{4,3,2,1,0:T(8,128)S(1)}, u32[]{:S(2)}, u32[]{:S(2)}) %all-to-all-start.2) | async-done | bytes 1179680 | tf_op jit(solution)/shard_map/all_to_all | solution.py:269
  259.8 3.8 %all_to_all.33 = f32[2,1,20480]{2,1,0:T(1,128)S(1)} all-to-all(f32[2,1,20480]{2,1,0:T(1,128)S(1)} %copy.120), channel_id=1, replica_groups=mesh['grp'=2,'gx'=8,'rep'=2] {'rep'}, dimensions={0} | all-to-all | bytes 327680 | tf_op jit(solution)/shard_map/all_to_all | solution.py:411
  267.7 11.0 %multiply_add_fusion = f32[8,32,2,32,32]{4,3,2,1,0:T(8,128)} fusion(f32[8,32,32]{2,1,0:T(8,128)S(1)} %copy.130, f32[8,32,2,32]{3,2,1,0:T(2,128)S(1)} %copy.129, f32[8,32,32]{2,1,0:T(8,128)S(1)} %copy.128, f32[8,32,2,32]{3,2,1,0:T(2,128)S(1)} %copy.127, f32[8,32,32]{2,1,0:T(8,128)S(1)} %copy.126, f32[8,32,2,32]{3,2,1,0:T(2,128)S(1)} %copy.125, ...), kind=kLoop, calls=%fused_computation | loop fusion | flops 3670016 | bytes 2490368 | tf_op jit(solution)/shard_map/add | solution.py:432
  (113 shorter events, 15.8 us)
Async XLA Ops:
  7.2 57.3 %all-gather.2.cloned.1.call-start = ((), (), s32[]{:S(2)}) async-start(), calls=%async_computation.5 | async-start | bytes 3145728 | tf_op jit(solution)/shard_map/all_gather | solution.py:320
  24.1 5.8 %copy-start.5 = (f32[8,16,2,8,128]{4,3,2,1,0:T(8,128)S(1)}, f32[8,16,2,8,128]{4,3,2,1,0:T(8,128)}, u32[]{:S(2)}) copy-start(f32[8,16,2,8,128]{4,3,2,1,0:T(8,128)} %shard_map.191) | copy-start | bytes 3145732
  24.1 38.6 %copy-start.1 = (f32[32,256]{1,0:T(8,128)S(1)}, f32[32,256]{1,0:T(8,128)}, u32[]{:S(2)}) copy-start(f32[32,256]{1,0:T(8,128)} %constant.49.clone.table_ref) | copy-start | bytes 98308
  67.1 1.8 copy-start
  67.7 6.9 %copy-start.15 = (bf16[32,32]{1,0:T(8,128)(2,1)S(1)}, bf16[32,32]{1,0:T(8,128)(2,1)}, u32[]{:S(2)}) copy-start(bf16[32,32]{1,0:T(8,128)(2,1)} %param.19) | copy-start | bytes 6148
  70.9 29.2 %all-to-all-start.1 = ((f32[8,16,2,8,128]{4,3,2,1,0:T(8,128)}), f32[8,16,2,8,128]{4,3,2,1,0:T(8,128)S(1)}, u32[]{:S(2)}, u32[]{:S(2)}) async-start(f32[8,16,2,8,128]{4,3,2,1,0:T(8,128)} %shard_map.193), calls=%async_computation.1 | async-start | bytes 2097152 | tf_op jit(solution)/shard_map/all_to_all | solution.py:269
  77.0 8.4 %copy-start.16 = (bf16[32,3]{0,1:T(4,128)(2,1)S(1)}, bf16[32,3]{0,1:T(4,128)(2,1)}, u32[]{:S(2)}) copy-start(bf16[32,3]{0,1:T(4,128)(2,1)} %param.20) | copy-start | bytes 580
  100.1 3.6 %copy-start.4 = (f32[8,16,2,8,128]{4,3,2,1,0:T(8,128)}, f32[8,16,2,8,128]{4,3,2,1,0:T(8,128)S(1)}, u32[]{:S(2)}) copy-start(f32[8,16,2,8,128]{4,3,2,1,0:T(8,128)S(1)} %all-to-all-done.1.m_ref) | copy-start | bytes 3145732
  100.1 127.1 %all-to-all-start.4 = ((f32[2,1,16384]{2,1,0:T(1,128)}), f32[2,1,16384]{2,1,0:T(1,128)S(1)}, u32[]{:S(2)}, u32[]{:S(2)}) async-start(f32[2,1,16384]{2,1,0:T(1,128)} %reshape.243), calls=%async_computation.4 | async-start | bytes 262144 | tf_op jit(solution)/shard_map/all_to_all | solution.py:308
  151.9 1.9 copy-start.3
  154.1 9.1 %copy-start.6 = (s32[1,16,128,128]{3,2,1,0:T(8,128)S(1)}, s32[1,16,128,128]{3,2,1,0:T(8,128)}, u32[]{:S(2)}) copy-start(s32[1,16,128,128]{3,2,1,0:T(8,128)} %param.18) | copy-start | bytes 3145732
  154.4 4.0 %collective-permute-start.1 = (bf16[1,128,128]{2,1,0:T(8,128)(2,1)S(1)}, bf16[1,128,128]{2,1,0:T(8,128)(2,1)S(1)}, u32[]{:S(2)}, u32[]{:S(2)}) collective-permute-start(bf16[1,128,128]{2,1,0:T(8,128)(2,1)S(1)} %get-tuple-element.51), channel_id=1, source_target_pairs={{2,0},{4,2},{6,4},{8,6},{10,8},{12,10},{14,12},{0,14},{3,1},{5,3},... | collective-permute-start | bytes 98312 | tf_op jit(solution)/shard_map/ppermute | solution.py:209
  156.5 6.6 %collective-permute-start = (bf16[1,128,128]{2,1,0:T(8,128)(2,1)S(1)}, bf16[1,128,128]{2,1,0:T(8,128)(2,1)S(1)}, u32[]{:S(2)}, u32[]{:S(2)}) collective-permute-start(bf16[1,128,128]{2,1,0:T(8,128)(2,1)S(1)} %get-tuple-element.50), channel_id=1, source_target_pairs={{0,2},{2,4},{4,6},{6,8},{8,10},{10,12},{12,14},{14,0},{1,3},{3,5},... | collective-permute-start | bytes 98312 | tf_op jit(solution)/shard_map/ppermute | solution.py:208
  165.0 1.0 copy-start.2
  165.0 1.3 copy-start.9
  166.3 4.8 %collective-permute-start.3 = (bf16[1,128,128]{2,1,0:T(8,128)(2,1)S(1)}, bf16[1,128,128]{2,1,0:T(8,128)(2,1)S(1)}, u32[]{:S(2)}, u32[]{:S(2)}) collective-permute-start(bf16[1,128,128]{2,1,0:T(8,128)(2,1)S(1)} %get-tuple-element.79), channel_id=1, source_target_pairs={{2,0},{4,2},{6,4},{8,6},{10,8},{12,10},{14,12},{0,14},{3,1},{5,3},... | collective-permute-start | bytes 98312 | tf_op jit(solution)/shard_map/ppermute | solution.py:209
  166.4 6.7 %collective-permute-start.2 = (bf16[1,128,128]{2,1,0:T(8,128)(2,1)S(1)}, bf16[1,128,128]{2,1,0:T(8,128)(2,1)S(1)}, u32[]{:S(2)}, u32[]{:S(2)}) collective-permute-start(bf16[1,128,128]{2,1,0:T(8,128)(2,1)S(1)} %get-tuple-element.78), channel_id=1, source_target_pairs={{0,2},{2,4},{4,6},{6,8},{8,10},{10,12},{12,14},{14,0},{1,3},{3,5},... | collective-permute-start | bytes 98312 | tf_op jit(solution)/shard_map/ppermute | solution.py:208
  171.1 3.2 %copy-start.7 = (f32[16,1,128,128]{3,2,1,0:T(8,128)S(1)}, f32[16,1,128,128]{3,2,1,0:T(8,128)}, u32[]{:S(2)}) copy-start(f32[16,1,128,128]{3,2,1,0:T(8,128)} %get-tuple-element.84) | copy-start | bytes 3145732
  171.1 3.2 %copy-start.8 = (f32[16,1,128,128]{3,2,1,0:T(8,128)S(1)}, f32[16,1,128,128]{3,2,1,0:T(8,128)}, u32[]{:S(2)}) copy-start(f32[16,1,128,128]{3,2,1,0:T(8,128)} %get-tuple-element.85) | copy-start | bytes 3145732
  171.1 3.2 %copy-start.10 = (bf16[1,16,3,128,128]{4,3,2,1,0:T(8,128)(2,1)S(1)}, bf16[1,16,3,128,128]{4,3,2,1,0:T(8,128)(2,1)}, u32[]{:S(2)}) copy-start(bf16[1,16,3,128,128]{4,3,2,1,0:T(8,128)(2,1)} %param.17) | copy-start | bytes 4718596
  177.0 44.4 %copy-start.11 = (f32[512,512]{1,0:T(8,128)S(1)}, f32[512,512]{1,0:T(8,128)}, u32[]{:S(2)}) copy-start(f32[512,512]{1,0:T(8,128)} %constant.53.clone) | copy-start | bytes 3145732
  177.0 44.4 %copy-start.12 = (f32[32,512]{1,0:T(8,128)S(1)}, f32[32,512]{1,0:T(8,128)}, u32[]{:S(2)}) copy-start(f32[32,512]{1,0:T(8,128)} %constant.51.clone) | copy-start | bytes 196612
  177.0 46.6 %copy-start.13 = (f32[512,48]{1,0:T(8,128)S(1)}, f32[512,48]{1,0:T(8,128)}, u32[]{:S(2)}) copy-start(f32[512,48]{1,0:T(8,128)} %constant.54.clone) | copy-start | bytes 294916
  177.0 47.9 %copy-start.14 = (f32[48,3]{1,0:T(8,128)S(1)}, f32[48,3]{1,0:T(8,128)}, u32[]{:S(2)}) copy-start(f32[48,3]{1,0:T(8,128)} %constant.52.clone) | copy-start | bytes 1732
  227.2 30.3 %all-to-all-start.2 = ((f32[8,18,2,8,128]{4,3,2,1,0:T(8,128)}), f32[8,18,2,8,128]{4,3,2,1,0:T(8,128)S(1)}, u32[]{:S(2)}, u32[]{:S(2)}) async-start(f32[8,18,2,8,128]{4,3,2,1,0:T(8,128)} %broadcast_dynamic-update-slice_fusion), calls=%async_computation.2 | async-start | bytes 2359296 | tf_op jit(solution)/shard_map/all_to_all | solution.py:269
Sparse Core Ops, SparseCore 0:
  30.0 13.2 all-gather.1
